TPU v7x, 512 devices: a whole 4x8x8 slice. The times are simulated.
512 devices in a mesh: seq: 32 (over x, z), exp: 16 (over y, core).
Axes of the slice: x: 4, y: 8, z: 8, core: 2. Of those that a mesh axis runs over, the one named last changes fastest.
Arguments:
- query_tok: bfloat16 [32768, 4096], P('seq', 'exp'), may hold values from -6 to 6
- key_tok: bfloat16 [32768, 4096], P('seq', 'exp'), may hold values from -6 to 6
- value_tok: bfloat16 [32768, 4096], P('seq', 'exp'), may hold values from -6 to 6
- grad_out: bfloat16 [32768, 4096], P('seq', 'exp'), may hold values from -6 to 6
- decay_rate: float32 [32], P('exp'), may hold values from 1.8626451e-07 to 0.025
Outputs:
- attended: bfloat16 [32768, 4096], P(('seq', 'exp'))
- query_gradient: bfloat16 [32768, 4096], P(('seq', 'exp'))
- key_gradient: bfloat16 [32768, 4096], P(('seq', 'exp'))
- value_gradient: bfloat16 [32768, 4096], P(('seq', 'exp'))
All inputs are finite; a program needn't handle non-finite values.
Results may differ from a plain program's by a relative error of at most 0.0048.
Values may be sent and summed in bfloat16 or wider, within the bound.
A program may use at most 64 MiB of HBM per device.

v0:
```python
import jax
import jax.numpy as jnp
from jax import lax
from jax.sharding import PartitionSpec as P


def carried_in(part, axis, combine, identity, reverse):
    count = lax.axis_size(axis)
    place = lax.axis_index(axis)
    ahead = count - 1 - place if reverse else place
    gathered = jax.tree.map(lambda a: lax.all_gather(a, axis), part)
    state = jax.tree.map(lambda a, e: jnp.zeros_like(a) + jnp.asarray(e, a.dtype), part, identity)

    def one(lap, state):
        source = count - 1 - lap if reverse else lap
        return combine(
            state, jax.tree.map(lambda a: lax.dynamic_index_in_dim(a, source, 0, False), gathered)
        )

    return lax.fori_loop(0, ahead, one, state)


def shortened(shard):

    def short(part):
        return part.astype(jnp.bfloat16) if part.dtype == jnp.float32 else part

    return jax.tree.map(short, shard)


def shards(query_tok, key_tok, value_tok, grad_out, decay_rate):
    greatest_precision = lax.Precision.HIGHEST
    seg_len = query_tok.shape[0]
    num_heads = decay_rate.shape[0]
    head_size = query_tok.shape[1] // num_heads
    total_len = seg_len * lax.axis_size("seq")
    scale_head = jnp.sqrt((2.0 * decay_rate + 2.0 / total_len) / head_size)
    shape_three = (seg_len, num_heads, head_size)
    query_heads = query_tok.reshape(shape_three)
    key_heads = key_tok.reshape(shape_three)
    value_heads = value_tok.reshape(shape_three)
    upstream = grad_out.reshape(shape_three)
    position = jnp.arange(seg_len, dtype=jnp.float32)
    to_end = jnp.exp(-decay_rate[None, :] * (seg_len - position[:, None]))
    from_start = jnp.exp(-decay_rate[None, :] * (position[:, None] + 1.0))
    key_product = (key_heads * to_end[:, :, None]).astype(jnp.bfloat16)
    query_product = (query_heads * from_start[:, :, None]).astype(jnp.bfloat16)
    dev_key = jnp.einsum(
        "ihd,ihe->hde", key_product, value_heads, preferred_element_type=jnp.float32
    )
    dev_query = jnp.einsum(
        "ihd,ihe->hde", query_product, upstream, preferred_element_type=jnp.float32
    )
    zero_state = jnp.zeros((num_heads, head_size, head_size), jnp.float32)
    piece_decay = jnp.exp(-decay_rate * seg_len)

    def chained(earlier, latter):
        return (earlier[0] * latter[0], latter[0][:, None, None] * earlier[1] + latter[1])

    identity = (jnp.ones((num_heads,), jnp.float32), zero_state)
    incoming = carried_in((piece_decay, dev_key), "seq", chained, identity, False)[1]
    outgoing = carried_in((piece_decay, dev_query), "seq", chained, identity, True)[1]
    offsets = position[:, None] - position[None, :]
    over_rows = (((0,), (0,)), ((), ()))
    over_cols = (((1,), (1,)), ((), ()))

    def head_work(index):
        rate = decay_rate[index]
        scale = scale_head[index]
        query_one = query_heads[:, index, :]
        key_one = key_heads[:, index, :]
        value_one = value_heads[:, index, :]
        upstream_one = upstream[:, index, :]
        start_state = incoming[index]
        end_state = outgoing[index]
        damping = jnp.where(offsets >= 0, jnp.exp(-rate * jnp.maximum(offsets, 0.0)), 0.0) * scale
        scores = lax.dot_general(query_one, key_one, over_cols, preferred_element_type=jnp.float32)
        weights = (scores * damping).astype(jnp.bfloat16)
        grad_scores = lax.dot_general(
            upstream_one, value_one, over_cols, preferred_element_type=jnp.float32
        )
        gweights = (grad_scores * damping).astype(jnp.bfloat16)
        leading_scale = (scale * jnp.exp(-rate * position))[:, None]
        trailing_scale = (scale * jnp.exp(-rate * (seg_len - 1.0 - position)))[:, None]
        attended = jnp.dot(weights, value_one, preferred_element_type=jnp.float32)
        attended = attended + leading_scale * jnp.dot(
            query_one.astype(jnp.float32), start_state, precision=greatest_precision
        )
        query_gradient = jnp.dot(gweights, key_one, preferred_element_type=jnp.float32)
        query_gradient = query_gradient + leading_scale * lax.dot_general(
            upstream_one.astype(jnp.float32), start_state, over_cols, precision=greatest_precision
        )
        key_gradient = lax.dot_general(
            gweights, query_one, over_rows, preferred_element_type=jnp.float32
        )
        key_gradient = key_gradient + trailing_scale * lax.dot_general(
            value_one.astype(jnp.float32), end_state, over_cols, precision=greatest_precision
        )
        value_gradient = lax.dot_general(
            weights, upstream_one, over_rows, preferred_element_type=jnp.float32
        )
        value_gradient = value_gradient + trailing_scale * jnp.dot(
            key_one.astype(jnp.float32), end_state, precision=greatest_precision
        )
        return (
            attended.astype(jnp.bfloat16),
            query_gradient.astype(jnp.bfloat16),
            key_gradient.astype(jnp.bfloat16),
            value_gradient.astype(jnp.bfloat16),
        )

    head_outputs = [head_work(index) for index in range(num_heads)]
    results = tuple(
        (
            jnp.stack([single[member] for single in head_outputs], axis=1).reshape(
                seg_len, num_heads * head_size
            )
            for member in range(4)
        )
    )
    return jax.tree.map(
        lambda part, own: part.astype(own.dtype),
        lax.all_to_all(shortened(results), "exp", split_axis=0, concat_axis=1, tiled=True),
        results,
    )


def solution(mesh):
    placed = (P("seq", "exp"), P("seq", "exp"), P("seq", "exp"), P("seq", "exp"), P("exp"))
    return jax.shard_map(
        shards,
        mesh=mesh,
        in_specs=placed,
        out_specs=(
            P(("seq", "exp"), None),
            P(("seq", "exp"), None),
            P(("seq", "exp"), None),
            P(("seq", "exp"), None),
        ),
        check_vma=False,
    )
```

profile of v0, /device:TPU:1, one launch (start us, length us, event | category | flops | bytes accessed | tf_op | source)
XLA Modules:
  0.0 307.9 jit_solution(5324452624342614884)
XLA Ops:
  18.3 67.7 %all-reduce = f32[64]{0:T(128)S(1)} all-reduce(f32[64]{0:T(128)S(1)} %get-tuple-element.161), channel_id=2, replica_groups=mesh['seq'=32,'exp'=16] {'seq'}, use_global_device_ids=true, to_apply=%add | all-reduce | flops 64 | bytes 512
  88.0 2.2 multiply_convert_fusion
  93.3 2.2 multiply_convert_fusion.1
  98.6 3.2 %multiply_convert_fusion.2 = bf16[1024,1024]{1,0:T(8,128)(2,1)S(1)} fusion(f32[]{:T(128)} %bitcast.20, f32[]{:T(128)} %bitcast.19, bf16[1024,2,128]{0,2,1:T(8,128)(2,1)S(1)} %bitcast.223, bf16[1024,2,128]{0,2,1:T(8,128)(2,1)} %bitcast.230), kind=kOutput, calls=%fused_computation.6 | convolution fusion | flops 276824064 | bytes 2622464 | tf_op jit(solution)/shard_map/dot_general | solution.py:77
  101.8 3.6 %multiply_convert_fusion.3 = bf16[1024,1024]{1,0:T(8,128)(2,1)} fusion(f32[]{:T(128)} %bitcast.9, f32[]{:T(128)} %bitcast.8, bf16[1024,2,128]{0,2,1:T(8,128)(2,1)S(1)} %bitcast.224, bf16[1024,2,128]{0,2,1:T(8,128)(2,1)S(1)} %bitcast.231), kind=kOutput, calls=%fused_computation.8 | convolution fusion | flops 276824064 | bytes 2621448 | tf_op jit(solution)/shard_map/dot_general | solution.py:77
  110.1 2.2 all_to_all.60
  112.3 22.3 %all-to-all-start.1 = ((bf16[16,64,256]{2,1,0:T(8,128)(2,1)}), bf16[16,64,256]{2,1,0:T(8,128)(2,1)}, u32[]{:S(2)}, u32[]{:S(2)}) async-start(bf16[16,64,256]{2,1,0:T(8,128)(2,1)} %all_to_all.60), calls=%async_computation.1 | async-start | bytes 1048576 | tf_op jit(solution)/shard_map/all_to_all | solution.py:123
  134.6 57.9 %all-gather.8.cloned.1.call-done = f32[64,128,128]{2,1,0:T(8,128)} async-done(((f32[2,128,128]{2,1,0:T(8,128)}), f32[64,128,128]{2,1,0:T(8,128)}) %all-gather.8.cloned.1.call-update) | async-done | bytes 4194320 | tf_op jit(solution)/shard_map/all_gather | solution.py:11
  192.5 32.2 %while.27 = (s32[]{:T(128)}, f32[2,128,128]{2,1,0:T(8,128)S(1)}, s32[]{:T(128)}, f32[32,2]{1,0:T(8,128)S(1)}, f32[32,2,128,128]{3,2,1,0:T(8,128)}, /*index=5*/s32[]{:T(128)}, s32[]{:T(128)}, s32[]{:T(128)}, s32[]{:T(128)}) while((s32[]{:T(128)}, f32[2,128,128]{2,1,0:T(8,128)S(1)}, s32[]{:T(128)}, f32[32,2]{1,0:T(8,128)S(1)}, ...), condition=%wide.region_3.4_spmd, body=%wide.region_2.3_spmd.sunk | while | flops 65542 | bytes 393395 | solution.py:20
  224.7 1.6 fusion.28
  226.3 1.6 fusion.29
  229.3 2.2 all_to_all.64
  231.5 10.8 %all-to-all-start.2 = ((bf16[16,64,256]{2,1,0:T(8,128)(2,1)}), bf16[16,64,256]{2,1,0:T(8,128)(2,1)}, u32[]{:S(2)}, u32[]{:S(2)}) async-start(bf16[16,64,256]{2,1,0:T(8,128)(2,1)} %all_to_all.64), calls=%async_computation.2 | async-start | bytes 1048576 | tf_op jit(solution)/shard_map/all_to_all | solution.py:123
  242.3 1.7 fusion.43
  243.9 2.3 fusion.40
  248.6 2.2 all_to_all.56
  250.8 8.9 %all-to-all-done.2 = bf16[16,64,256]{2,1,0:T(8,128)(2,1)} async-done(((bf16[16,64,256]{2,1,0:T(8,128)(2,1)}), bf16[16,64,256]{2,1,0:T(8,128)(2,1)}, u32[]{:S(2)}, u32[]{:S(2)}) %all-to-all-start.2) | async-done | bytes 524320 | tf_op jit(solution)/shard_map/all_to_all | solution.py:123
  259.7 4.1 %all-to-all-start = ((bf16[16,64,256]{2,1,0:T(8,128)(2,1)}), bf16[16,64,256]{2,1,0:T(8,128)(2,1)}, u32[]{:S(2)}, u32[]{:S(2)}) async-start(bf16[16,64,256]{2,1,0:T(8,128)(2,1)} %all_to_all.56), calls=%async_computation | async-start | bytes 1048576 | tf_op jit(solution)/shard_map/all_to_all | solution.py:123
  268.9 11.1 %all-to-all-done = bf16[16,64,256]{2,1,0:T(8,128)(2,1)} async-done(((bf16[16,64,256]{2,1,0:T(8,128)(2,1)}), bf16[16,64,256]{2,1,0:T(8,128)(2,1)}, u32[]{:S(2)}, u32[]{:S(2)}) %all-to-all-start) | async-done | bytes 524320 | tf_op jit(solution)/shard_map/all_to_all | solution.py:123
  280.0 3.5 %all-to-all-start.3 = ((bf16[16,64,256]{2,1,0:T(8,128)(2,1)}), bf16[16,64,256]{2,1,0:T(8,128)(2,1)S(1)}, u32[]{:S(2)}, u32[]{:S(2)}) async-start(bf16[16,64,256]{2,1,0:T(8,128)(2,1)} %all_to_all.68), calls=%async_computation.3 | async-start | bytes 1048576 | tf_op jit(solution)/shard_map/all_to_all | solution.py:123
  283.5 1.9 copy.106
  285.4 1.9 copy.107
  287.2 1.9 copy.105
  289.1 11.1 %all-to-all-done.3 = bf16[16,64,256]{2,1,0:T(8,128)(2,1)S(1)} async-done(((bf16[16,64,256]{2,1,0:T(8,128)(2,1)}), bf16[16,64,256]{2,1,0:T(8,128)(2,1)S(1)}, u32[]{:S(2)}, u32[]{:S(2)}) %all-to-all-start.3) | async-done | bytes 524320 | tf_op jit(solution)/shard_map/all_to_all | solution.py:123
  (123 shorter events, 62.5 us)
Async XLA Ops:
  7.2 9.2 %copy-start.6 = (f32[2]{0:T(128)S(1)}, f32[2]{0:T(128)}, u32[]{:S(2)}) copy-start(f32[2]{0:T(128)} %param.13) | copy-start | bytes 28
  7.2 8.0 %copy-start.5 = (bf16[1024,256]{1,0:T(8,128)(2,1)S(1)}, bf16[1024,256]{1,0:T(8,128)(2,1)}, u32[]{:S(2)}) copy-start(bf16[1024,256]{1,0:T(8,128)(2,1)} %param.12) | copy-start | bytes 1572868
  7.2 98.3 %all-gather.6.cloned.1.call-start = ((), (), s32[]{:S(2)}) async-start(), calls=%async_computation.4 | async-start | bytes 4325376 | tf_op jit(solution)/shard_map/all_gather | solution.py:11
  8.6 88.5 %copy-start.1 = (bf16[1024,256]{0,1:T(8,128)(2,1)}, bf16[1024,256]{0,1:T(8,128)(2,1)S(1)}, u32[]{:S(2)}) copy-start(bf16[1024,256]{0,1:T(8,128)(2,1)S(1)} %copy.67) | copy-start | bytes 1572868
  10.0 83.3 %copy-start.4 = (bf16[1024,256]{0,1:T(8,128)(2,1)}, bf16[1024,256]{0,1:T(8,128)(2,1)S(1)}, u32[]{:S(2)}) copy-start(bf16[1024,256]{0,1:T(8,128)(2,1)S(1)} %copy.69) | copy-start | bytes 1572868
  13.8 178.7 %all-gather.8.cloned.1.call-start = ((), (), s32[]{:S(2)}) async-start(), calls=%async_computation.5 | async-start | bytes 4325376 | tf_op jit(solution)/shard_map/all_gather | solution.py:11
  98.6 3.2 %copy-start.2 = (bf16[1024,256]{0,1:T(8,128)(2,1)S(1)}, bf16[1024,256]{0,1:T(8,128)(2,1)}, u32[]{:S(2)}) copy-start(bf16[1024,256]{0,1:T(8,128)(2,1)} %copy-done.1) | copy-start | bytes 1572868
  112.3 119.2 %all-to-all-start.1 = ((bf16[16,64,256]{2,1,0:T(8,128)(2,1)}), bf16[16,64,256]{2,1,0:T(8,128)(2,1)}, u32[]{:S(2)}, u32[]{:S(2)}) async-start(bf16[16,64,256]{2,1,0:T(8,128)(2,1)} %all_to_all.60), calls=%async_computation.1 | async-start | bytes 1048576 | tf_op jit(solution)/shard_map/all_to_all | solution.py:123
  231.5 28.2 %all-to-all-start.2 = ((bf16[16,64,256]{2,1,0:T(8,128)(2,1)}), bf16[16,64,256]{2,1,0:T(8,128)(2,1)}, u32[]{:S(2)}, u32[]{:S(2)}) async-start(bf16[16,64,256]{2,1,0:T(8,128)(2,1)} %all_to_all.64), calls=%async_computation.2 | async-start | bytes 1048576 | tf_op jit(solution)/shard_map/all_to_all | solution.py:123
  259.7 20.3 %all-to-all-start = ((bf16[16,64,256]{2,1,0:T(8,128)(2,1)}), bf16[16,64,256]{2,1,0:T(8,128)(2,1)}, u32[]{:S(2)}, u32[]{:S(2)}) async-start(bf16[16,64,256]{2,1,0:T(8,128)(2,1)} %all_to_all.56), calls=%async_computation | async-start | bytes 1048576 | tf_op jit(solution)/shard_map/all_to_all | solution.py:123
  263.9 1.6 copy-start
  263.9 2.3 copy-start.3
  280.0 20.2 %all-to-all-start.3 = ((bf16[16,64,256]{2,1,0:T(8,128)(2,1)}), bf16[16,64,256]{2,1,0:T(8,128)(2,1)S(1)}, u32[]{:S(2)}, u32[]{:S(2)}) async-start(bf16[16,64,256]{2,1,0:T(8,128)(2,1)} %all_to_all.68), calls=%async_computation.3 | async-start | bytes 1048576 | tf_op jit(solution)/shard_map/all_to_all | solution.py:123
Sparse Core Ops, SparseCore 0:
  14.0 90.7 all-gather.5
  107.9 84.5 all-gather.7
where the time goes:
time: 310 us; the launch traced here: 308 us
  waiting for transfers between devices  89.1 us (29%)
  blocking collectives  67.7 us (22%)
  starting transfers between devices  40.8 us (13%)
  other arithmetic  33.3 us (11%)
  matrix products  32.9 us (11%)
  local copies, waits for them, and re-layouts  26.6 us (9%)
  between operations  16.3 us (5%)
    unnamed x1, blocking collectives  67.7 us
    all_gather x2, waiting for transfers between devices, carried_in(): gathered = jax.tree.map(lambda a: lax.all_gather(a, axis), part)  57.9 us
    all_to_all x4, starting transfers between devices, shards(): lax.all_to_all(shortened(results), 'exp', split_axis=0, concat_axis=1, ti...  40.7 us
    all_to_all x4, waiting for transfers between devices, shards(): lax.all_to_all(shortened(results), 'exp', split_axis=0, concat_axis=1, ti...  31.2 us
    add x31, other arithmetic, chained(): latter[0][:, None, None] * earlier[1] + latter[1]  30.9 us
    all_to_all x8, local copies, waits for them, and re-layouts, shards(): lax.all_to_all(shortened(results), 'exp', split_axis=0, concat_axis=1, ti...  14.1 us
    dot_general x2, matrix products, head_work(): lax.dot_general(query_one, key_one, over_cols, preferred_element_type=jnp...  6.83 us
    unnamed x20, local copies, waits for them, and re-layouts  6.36 us
  transfers between devices with their start and end apart: 6, of which 4 were waited for; matrix products, arithmetic and copies ran while one was open for 25% of the time, Pallas kernels for 0%

commit v1 on v0

--- a/solution.py
+++ b/solution.py
@@ -4,28 +4,32 @@
 from jax.sharding import PartitionSpec as P
 
 
-def carried_in(part, axis, combine, identity, reverse):
+def decayed_scan(part, rate_len, axis, reverse):
     count = lax.axis_size(axis)
     place = lax.axis_index(axis)
     ahead = count - 1 - place if reverse else place
-    gathered = jax.tree.map(lambda a: lax.all_gather(a, axis), part)
-    state = jax.tree.map(lambda a, e: jnp.zeros_like(a) + jnp.asarray(e, a.dtype), part, identity)
+    sign = -1 if reverse else 1
 
-    def one(lap, state):
-        source = count - 1 - lap if reverse else lap
-        return combine(
-            state, jax.tree.map(lambda a: lax.dynamic_index_in_dim(a, source, 0, False), gathered)
-        )
+    def shifted(x, d):
+        pairs = [(s, s + sign * d) for s in range(count) if 0 <= s + sign * d < count]
+        return lax.ppermute(x, axis, pairs)
 
-    return lax.fori_loop(0, ahead, one, state)
+    def weight(d):
+        return jnp.exp(-rate_len * d)[:, None, None]
 
-
-def shortened(shard):
-
-    def short(part):
-        return part.astype(jnp.bfloat16) if part.dtype == jnp.float32 else part
-
-    return jax.tree.map(short, shard)
+    total = part
+    d = 1
+    while 2 * d < count:
+        got = shifted(total, d)
+        total = total + jnp.where(ahead >= d, weight(d), 0.0) * got
+        d *= 2
+    near = shifted(total, 1)
+    far_d = d + 1
+    result = jnp.where(ahead >= 1, 1.0, 0.0) * near
+    if far_d < count:
+        far = shifted(total, far_d)
+        result = result + jnp.where(ahead >= far_d, weight(d), 0.0) * far
+    return result
 
 
 def shards(query_tok, key_tok, value_tok, grad_out, decay_rate):
@@ -51,15 +55,9 @@
     dev_query = jnp.einsum(
         "ihd,ihe->hde", query_product, upstream, preferred_element_type=jnp.float32
     )
-    zero_state = jnp.zeros((num_heads, head_size, head_size), jnp.float32)
-    piece_decay = jnp.exp(-decay_rate * seg_len)
-
-    def chained(earlier, latter):
-        return (earlier[0] * latter[0], latter[0][:, None, None] * earlier[1] + latter[1])
-
-    identity = (jnp.ones((num_heads,), jnp.float32), zero_state)
-    incoming = carried_in((piece_decay, dev_key), "seq", chained, identity, False)[1]
-    outgoing = carried_in((piece_decay, dev_query), "seq", chained, identity, True)[1]
+    rate_len = decay_rate * seg_len
+    incoming = decayed_scan(dev_key, rate_len, "seq", False)
+    outgoing = decayed_scan(dev_query, rate_len, "seq", True)
     offsets = position[:, None] - position[None, :]
     over_rows = (((0,), (0,)), ((), ()))
     over_cols = (((1,), (1,)), ((), ()))
@@ -118,11 +116,7 @@
             for member in range(4)
         )
     )
-    return jax.tree.map(
-        lambda part, own: part.astype(own.dtype),
-        lax.all_to_all(shortened(results), "exp", split_axis=0, concat_axis=1, tiled=True),
-        results,
-    )
+    return lax.all_to_all(results, "exp", split_axis=0, concat_axis=1, tiled=True)
 
 
 def solution(mesh):

time: 310 us -> 192 us (0.62)
  the two profiles are of different devices: /device:TPU:1 before, /device:TPU:7 now
where the time goes in v1:
time: 192 us; the launch traced here: 191 us
  starting transfers between devices  65.7 us (34%)
  waiting for transfers between devices  58.9 us (31%)
  matrix products  27.8 us (14%)
  local copies, waits for them, and re-layouts  24.9 us (13%)
  other arithmetic  11 us (6%)
  between operations  2.55 us (1%)
    ppermute x12, starting transfers between devices, shifted(): return lax.ppermute(x, axis, pairs)  41.6 us
    all_to_all x4, waiting for transfers between devices, shards(): lax.all_to_all(results, 'exp', split_axis=0, concat_axis=1, tiled=True)  32.3 us
    ppermute x12, waiting for transfers between devices, shifted(): return lax.ppermute(x, axis, pairs)  26.6 us
    all_to_all x4, starting transfers between devices, shards(): lax.all_to_all(results, 'exp', split_axis=0, concat_axis=1, tiled=True)  24.2 us
    all_to_all x8, local copies, waits for them, and re-layouts, shards(): lax.all_to_all(results, 'exp', split_axis=0, concat_axis=1, tiled=True)  14.1 us
    add x8, other arithmetic, decayed_scan(): total = total + jnp.where(ahead >= d, weight(d), 0.0) * got  6.3 us
    dot_general x2, matrix products, head_work(): lax.dot_general(query_one, key_one, over_cols, preferred_element_type=jnp...  5.76 us
    dot_general x2, matrix products, head_work(): lax.dot_general(upstream_one, value_one, over_cols, preferred_element_typ...  5.29 us
  transfers between devices with their start and end apart: 16, of which 9 were waited for; matrix products, arithmetic and copies ran while one was open for 26% of the time, Pallas kernels for 0%

profile of v1, /device:TPU:7, one launch (start us, length us, event | category | flops | bytes accessed | tf_op | source)
XLA Modules:
  0.0 190.9 jit_solution(13987739689823969077)
XLA Ops:
  4.6 4.0 %collective-permute-start = (f32[2,128,128]{2,1,0:T(8,128)S(1)}, f32[2,128,128]{2,1,0:T(8,128)}, u32[]{:S(2)}, u32[]{:S(2)}) collective-permute-start(f32[2,128,128]{2,1,0:T(8,128)S(1)} %fusion.34), channel_id=1, source_target_pairs={{0,16},{16,32},{32,48},{48,64},{64,80},{80,96},{96,112},{112,128},... | collective-permute-start | bytes 393224 | tf_op jit(solution)/shard_map/ppermute | solution.py:15
  9.4 8.9 %collective-permute-start.6 = (f32[2,128,128]{2,1,0:T(8,128)S(1)}, f32[2,128,128]{2,1,0:T(8,128)S(1)}, u32[]{:S(2)}, u32[]{:S(2)}) collective-permute-start(f32[2,128,128]{2,1,0:T(8,128)S(1)} %fusion.35), channel_id=1, source_target_pairs={{16,0},{32,16},{48,32},{64,48},{80,64},{96,80},{112,96},{128,112},... | collective-permute-start | bytes 393224 | tf_op jit(solution)/shard_map/ppermute | solution.py:15
  20.2 3.2 %multiply_convert_fusion = bf16[1024,1024]{1,0:T(8,128)(2,1)S(1)} fusion(f32[]{:T(128)} %bitcast.14, f32[]{:T(128)} %bitcast.13, bf16[1024,2,128]{0,2,1:T(8,128)(2,1)} %bitcast.212, bf16[1024,2,128]{0,2,1:T(8,128)(2,1)S(1)} %bitcast.191), kind=kOutput, calls=%fused_computation | convolution fusion | flops 276824064 | bytes 2622464 | tf_op jit(solution)/shard_map/dot_general | solution.py:77
  26.4 2.3 %multiply_convert_fusion.2 = bf16[1024,1024]{1,0:T(8,128)(2,1)S(1)} fusion(f32[]{:T(128)} %bitcast.14, f32[]{:T(128)} %bitcast.13, bf16[1024,2,128]{0,2,1:T(8,128)(2,1)S(1)} %bitcast.199, bf16[1024,2,128]{0,2,1:T(8,128)(2,1)S(1)} %bitcast.206), kind=kOutput, calls=%fused_computation.2 | convolution fusion | flops 276824064 | bytes 2621448 | tf_op jit(solution)/shard_map/dot_general | solution.py:75
  29.4 2.1 %multiply_convert_fusion.1 = bf16[1024,1024]{1,0:T(8,128)(2,1)S(1)} fusion(f32[]{:T(128)} %bitcast.5, f32[]{:T(128)} %bitcast.4, bf16[1024,2,128]{0,2,1:T(8,128)(2,1)S(1)} %bitcast.216, bf16[1024,2,128]{0,2,1:T(8,128)(2,1)S(1)} %bitcast.192), kind=kOutput, calls=%fused_computation.1 | convolution fusion | flops 276824064 | bytes 2621448 | tf_op jit(solution)/shard_map/dot_general | solution.py:77
  31.5 3.5 %multiply_convert_fusion.3 = bf16[1024,1024]{1,0:T(8,128)(2,1)} fusion(f32[]{:T(128)} %bitcast.5, f32[]{:T(128)} %bitcast.4, bf16[1024,2,128]{0,2,1:T(8,128)(2,1)S(1)} %bitcast.200, bf16[1024,2,128]{0,2,1:T(8,128)(2,1)S(1)} %bitcast.207), kind=kOutput, calls=%fused_computation.4 | convolution fusion | flops 276824064 | bytes 2621448 | tf_op jit(solution)/shard_map/dot_general | solution.py:75
  39.1 1.9 %collective-permute-start.1 = (f32[2,128,128]{2,1,0:T(8,128)S(1)}, f32[2,128,128]{2,1,0:T(8,128)}, u32[]{:S(2)}, u32[]{:S(2)}) collective-permute-start(f32[2,128,128]{2,1,0:T(8,128)S(1)} %multiply_add_fusion.9), channel_id=1, source_target_pairs={{0,32},{16,48},{32,64},{48,80},{64,96},{80,112},{96,128},{112,144}... | collective-permute-start | bytes 393224 | tf_op jit(solution)/shard_map/ppermute | solution.py:15
  42.4 9.3 %collective-permute-done.1 = f32[2,128,128]{2,1,0:T(8,128)} collective-permute-done((f32[2,128,128]{2,1,0:T(8,128)S(1)}, f32[2,128,128]{2,1,0:T(8,128)}, u32[]{:S(2)}, u32[]{:S(2)}) %collective-permute-start.1) | collective-permute-done | bytes 131104 | tf_op jit(solution)/shard_map/ppermute | solution.py:15
  55.4 1.9 %collective-permute-start.7 = (f32[2,128,128]{2,1,0:T(8,128)S(1)}, f32[2,128,128]{2,1,0:T(8,128)S(1)}, u32[]{:S(2)}, u32[]{:S(2)}) collective-permute-start(f32[2,128,128]{2,1,0:T(8,128)S(1)} %multiply_add_fusion.4), channel_id=1, source_target_pairs={{32,0},{48,16},{64,32},{80,48},{96,64},{112,80},{128,96},{144,112}... | collective-permute-start | bytes 393224 | tf_op jit(solution)/shard_map/ppermute | solution.py:15
  57.3 7.6 %collective-permute-done.2 = f32[2,128,128]{2,1,0:T(8,128)S(1)} collective-permute-done((f32[2,128,128]{2,1,0:T(8,128)S(1)}, f32[2,128,128]{2,1,0:T(8,128)S(1)}, u32[]{:S(2)}, u32[]{:S(2)}) %collective-permute-start.2) | collective-permute-done | bytes 131104 | tf_op jit(solution)/shard_map/ppermute | solution.py:15
  67.6 5.1 %collective-permute-start.8 = (f32[2,128,128]{2,1,0:T(8,128)S(1)}, f32[2,128,128]{2,1,0:T(8,128)S(1)}, u32[]{:S(2)}, u32[]{:S(2)}) collective-permute-start(f32[2,128,128]{2,1,0:T(8,128)S(1)} %multiply_add_fusion.3), channel_id=1, source_target_pairs={{64,0},{80,16},{96,32},{112,48},{128,64},{144,80},{160,96},{176,11... | collective-permute-start | bytes 393224 | tf_op jit(solution)/shard_map/ppermute | solution.py:15
  78.1 4.2 %collective-permute-start.9 = (f32[2,128,128]{2,1,0:T(8,128)S(1)}, f32[2,128,128]{2,1,0:T(8,128)S(1)}, u32[]{:S(2)}, u32[]{:S(2)}) collective-permute-start(f32[2,128,128]{2,1,0:T(8,128)S(1)} %multiply_add_fusion.2), channel_id=1, source_target_pairs={{128,0},{144,16},{160,32},{176,48},{192,64},{208,80},{224,96},{240... | collective-permute-start | bytes 393224 | tf_op jit(solution)/shard_map/ppermute | solution.py:15
  87.4 2.2 %all_to_all.60 = bf16[16,64,256]{2,1,0:T(8,128)(2,1)} reshape(bf16[1024,2,128]{2,1,0:T(2,128)(2,1)} %copy.54) | data formatting | bytes 1048576 | tf_op jit(solution)/shard_map/all_to_all | solution.py:119
  89.6 8.7 %all-to-all-start.1 = ((bf16[16,64,256]{2,1,0:T(8,128)(2,1)}), bf16[16,64,256]{2,1,0:T(8,128)(2,1)}, u32[]{:S(2)}, u32[]{:S(2)}) async-start(bf16[16,64,256]{2,1,0:T(8,128)(2,1)} %all_to_all.60), calls=%async_computation.1 | async-start | bytes 1048576 | tf_op jit(solution)/shard_map/all_to_all | solution.py:119
  99.1 7.3 %collective-permute-start.11 = (f32[2,128,128]{2,1,0:T(8,128)}, f32[2,128,128]{2,1,0:T(8,128)S(1)}, u32[]{:S(2)}, u32[]{:S(2)}) collective-permute-start(f32[2,128,128]{2,1,0:T(8,128)} %multiply_add_fusion.1), channel_id=1, source_target_pairs={{272,0},{288,16},{304,32},{320,48},{336,64},{352,80},{368,96},{384... | collective-permute-start | bytes 393224 | tf_op jit(solution)/shard_map/ppermute | solution.py:15
  109.6 6.3 %collective-permute-done.10 = f32[2,128,128]{2,1,0:T(8,128)S(1)} collective-permute-done((f32[2,128,128]{2,1,0:T(8,128)}, f32[2,128,128]{2,1,0:T(8,128)S(1)}, u32[]{:S(2)}, u32[]{:S(2)}) %collective-permute-start.10) | collective-permute-done | bytes 131104 | tf_op jit(solution)/shard_map/ppermute | solution.py:15
  122.2 2.2 %all_to_all.64 = bf16[16,64,256]{2,1,0:T(8,128)(2,1)} reshape(bf16[1024,2,128]{2,1,0:T(2,128)(2,1)} %copy.59) | data formatting | bytes 1048576 | tf_op jit(solution)/shard_map/all_to_all | solution.py:119
  124.3 7.8 %all-to-all-start.2 = ((bf16[16,64,256]{2,1,0:T(8,128)(2,1)}), bf16[16,64,256]{2,1,0:T(8,128)(2,1)}, u32[]{:S(2)}, u32[]{:S(2)}) async-start(bf16[16,64,256]{2,1,0:T(8,128)(2,1)} %all_to_all.64), calls=%async_computation.2 | async-start | bytes 1048576 | tf_op jit(solution)/shard_map/all_to_all | solution.py:119
  137.1 2.2 %all_to_all.56 = bf16[16,64,256]{2,1,0:T(8,128)(2,1)} reshape(bf16[1024,2,128]{2,1,0:T(2,128)(2,1)} %copy.47) | data formatting | bytes 1048576 | tf_op jit(solution)/shard_map/all_to_all | solution.py:119
  139.2 10.3 %all-to-all-done.2 = bf16[16,64,256]{2,1,0:T(8,128)(2,1)} async-done(((bf16[16,64,256]{2,1,0:T(8,128)(2,1)}), bf16[16,64,256]{2,1,0:T(8,128)(2,1)}, u32[]{:S(2)}, u32[]{:S(2)}) %all-to-all-start.2) | async-done | bytes 524320 | tf_op jit(solution)/shard_map/all_to_all | solution.py:119
  149.6 4.1 %all-to-all-start = ((bf16[16,64,256]{2,1,0:T(8,128)(2,1)}), bf16[16,64,256]{2,1,0:T(8,128)(2,1)}, u32[]{:S(2)}, u32[]{:S(2)}) async-start(bf16[16,64,256]{2,1,0:T(8,128)(2,1)} %all_to_all.56), calls=%async_computation | async-start | bytes 1048576 | tf_op jit(solution)/shard_map/all_to_all | solution.py:119
  159.1 10.8 %all-to-all-done = bf16[16,64,256]{2,1,0:T(8,128)(2,1)} async-done(((bf16[16,64,256]{2,1,0:T(8,128)(2,1)}), bf16[16,64,256]{2,1,0:T(8,128)(2,1)}, u32[]{:S(2)}, u32[]{:S(2)}) %all-to-all-start) | async-done | bytes 524320 | tf_op jit(solution)/shard_map/all_to_all | solution.py:119
  169.9 3.5 %all-to-all-start.3 = ((bf16[16,64,256]{2,1,0:T(8,128)(2,1)}), bf16[16,64,256]{2,1,0:T(8,128)(2,1)S(1)}, u32[]{:S(2)}, u32[]{:S(2)}) async-start(bf16[16,64,256]{2,1,0:T(8,128)(2,1)} %all_to_all.68), calls=%async_computation.3 | async-start | bytes 1048576 | tf_op jit(solution)/shard_map/all_to_all | solution.py:119
  179.0 11.1 %all-to-all-done.3 = bf16[16,64,256]{2,1,0:T(8,128)(2,1)S(1)} async-done(((bf16[16,64,256]{2,1,0:T(8,128)(2,1)}), bf16[16,64,256]{2,1,0:T(8,128)(2,1)S(1)}, u32[]{:S(2)}, u32[]{:S(2)}) %all-to-all-start.3) | async-done | bytes 524320 | tf_op jit(solution)/shard_map/all_to_all | solution.py:119
  (101 shorter events, 57.9 us)
Async XLA Ops:
  0.6 2.9 %copy-start.15 = (f32[2]{0:T(128)S(1)}, f32[2]{0:T(128)}, u32[]{:S(2)}) copy-start(f32[2]{0:T(128)} %param.9) | copy-start | bytes 28
  0.6 8.0 %copy-start.10 = (bf16[1024,256]{1,0:T(8,128)(2,1)S(1)}, bf16[1024,256]{1,0:T(8,128)(2,1)}, u32[]{:S(2)}) copy-start(bf16[1024,256]{1,0:T(8,128)(2,1)} %param.5) | copy-start | bytes 1572868
  0.7 8.2 %copy-start.11 = (bf16[1024,256]{1,0:T(8,128)(2,1)S(1)}, bf16[1024,256]{1,0:T(8,128)(2,1)}, u32[]{:S(2)}) copy-start(bf16[1024,256]{1,0:T(8,128)(2,1)} %param.8) | copy-start | bytes 1572868
  2.0 6.6 %copy-start.2 = (bf16[1024,256]{0,1:T(8,128)(2,1)}, bf16[1024,256]{0,1:T(8,128)(2,1)S(1)}, u32[]{:S(2)}) copy-start(bf16[1024,256]{0,1:T(8,128)(2,1)S(1)} %copy.37) | copy-start | bytes 1572868
  4.6 18.7 %copy-start.13 = (f32[2,128,128]{2,1,0:T(8,128)}, f32[2,128,128]{2,1,0:T(8,128)S(1)}, u32[]{:S(2)}) copy-start(f32[2,128,128]{2,1,0:T(8,128)S(1)} %fusion.34) | copy-start | bytes 393220
  4.6 33.4 %collective-permute-start = (f32[2,128,128]{2,1,0:T(8,128)S(1)}, f32[2,128,128]{2,1,0:T(8,128)}, u32[]{:S(2)}, u32[]{:S(2)}) collective-permute-start(f32[2,128,128]{2,1,0:T(8,128)S(1)} %fusion.34), channel_id=1, source_target_pairs={{0,16},{16,32},{32,48},{48,64},{64,80},{80,96},{96,112},{112,128},... | collective-permute-start | bytes 393224 | tf_op jit(solution)/shard_map/ppermute | solution.py:15
  9.4 45.2 %collective-permute-start.6 = (f32[2,128,128]{2,1,0:T(8,128)S(1)}, f32[2,128,128]{2,1,0:T(8,128)S(1)}, u32[]{:S(2)}, u32[]{:S(2)}) collective-permute-start(f32[2,128,128]{2,1,0:T(8,128)S(1)} %fusion.35), channel_id=1, source_target_pairs={{16,0},{32,16},{48,32},{64,48},{80,64},{96,80},{112,96},{128,112},... | collective-permute-start | bytes 393224 | tf_op jit(solution)/shard_map/ppermute | solution.py:15
  26.4 2.9 %copy-start.6 = (bf16[1024,256]{0,1:T(8,128)(2,1)S(1)}, bf16[1024,256]{0,1:T(8,128)(2,1)}, u32[]{:S(2)}) copy-start(bf16[1024,256]{0,1:T(8,128)(2,1)} %copy-done.5) | copy-start | bytes 1572868
  39.1 12.6 %collective-permute-start.1 = (f32[2,128,128]{2,1,0:T(8,128)S(1)}, f32[2,128,128]{2,1,0:T(8,128)}, u32[]{:S(2)}, u32[]{:S(2)}) collective-permute-start(f32[2,128,128]{2,1,0:T(8,128)S(1)} %multiply_add_fusion.9), channel_id=1, source_target_pairs={{0,32},{16,48},{32,64},{48,80},{64,96},{80,112},{96,128},{112,144}... | collective-permute-start | bytes 393224 | tf_op jit(solution)/shard_map/ppermute | solution.py:15
  41.6 43.5 %copy-start.8 = (f32[1024,128]{1,0:T(8,128)S(1)}, f32[1024,128]{1,0:T(8,128)}, u32[]{:S(2)}) copy-start(f32[1024,128]{1,0:T(8,128)} %fusion.42) | copy-start | bytes 1572868
  41.6 43.9 %copy-start.9 = (f32[1024,128]{1,0:T(8,128)S(1)}, f32[1024,128]{1,0:T(8,128)}, u32[]{:S(2)}) copy-start(f32[1024,128]{1,0:T(8,128)} %fusion.39) | copy-start | bytes 1572868
  52.7 12.2 %collective-permute-start.2 = (f32[2,128,128]{2,1,0:T(8,128)S(1)}, f32[2,128,128]{2,1,0:T(8,128)S(1)}, u32[]{:S(2)}, u32[]{:S(2)}) collective-permute-start(f32[2,128,128]{2,1,0:T(8,128)S(1)} %multiply_add_fusion.8), channel_id=1, source_target_pairs={{0,64},{16,80},{32,96},{48,112},{64,128},{80,144},{96,160},{112,17... | collective-permute-start | bytes 393224 | tf_op jit(solution)/shard_map/ppermute | solution.py:15
  55.4 11.5 %collective-permute-start.7 = (f32[2,128,128]{2,1,0:T(8,128)S(1)}, f32[2,128,128]{2,1,0:T(8,128)S(1)}, u32[]{:S(2)}, u32[]{:S(2)}) collective-permute-start(f32[2,128,128]{2,1,0:T(8,128)S(1)} %multiply_add_fusion.4), channel_id=1, source_target_pairs={{32,0},{48,16},{64,32},{80,48},{96,64},{112,80},{128,96},{144,112}... | collective-permute-start | bytes 393224 | tf_op jit(solution)/shard_map/ppermute | solution.py:15
  65.6 7.1 %collective-permute-start.3 = (f32[2,128,128]{2,1,0:T(8,128)S(1)}, f32[2,128,128]{2,1,0:T(8,128)S(1)}, u32[]{:S(2)}, u32[]{:S(2)}) collective-permute-start(f32[2,128,128]{2,1,0:T(8,128)S(1)} %multiply_add_fusion.7), channel_id=1, source_target_pairs={{0,128},{16,144},{32,160},{48,176},{64,192},{80,208},{96,224},{112... | collective-permute-start | bytes 393224 | tf_op jit(solution)/shard_map/ppermute | solution.py:15
  67.6 9.7 %collective-permute-start.8 = (f32[2,128,128]{2,1,0:T(8,128)S(1)}, f32[2,128,128]{2,1,0:T(8,128)S(1)}, u32[]{:S(2)}, u32[]{:S(2)}) collective-permute-start(f32[2,128,128]{2,1,0:T(8,128)S(1)} %multiply_add_fusion.3), channel_id=1, source_target_pairs={{64,0},{80,16},{96,32},{112,48},{128,64},{144,80},{160,96},{176,11... | collective-permute-start | bytes 393224 | tf_op jit(solution)/shard_map/ppermute | solution.py:15
  73.4 10.3 %collective-permute-start.5 = (f32[2,128,128]{2,1,0:T(8,128)S(1)}, f32[2,128,128]{2,1,0:T(8,128)S(1)}, u32[]{:S(2)}, u32[]{:S(2)}) collective-permute-start(f32[2,128,128]{2,1,0:T(8,128)S(1)} %multiply_add_fusion.6), channel_id=1, source_target_pairs={{0,272},{16,288},{32,304},{48,320},{64,336},{80,352},{96,368},{112... | collective-permute-start | bytes 393224 | tf_op jit(solution)/shard_map/ppermute | solution.py:15
  74.7 10.3 %collective-permute-start.4 = (f32[2,128,128]{2,1,0:T(8,128)S(1)}, f32[2,128,128]{2,1,0:T(8,128)S(1)}, u32[]{:S(2)}, u32[]{:S(2)}) collective-permute-start(f32[2,128,128]{2,1,0:T(8,128)S(1)} %multiply_add_fusion.6), channel_id=1, source_target_pairs={{0,16},{16,32},{32,48},{48,64},{64,80},{80,96},{96,112},{112,128},... | collective-permute-start | bytes 393224 | tf_op jit(solution)/shard_map/ppermute | solution.py:15
  78.1 20.2 %collective-permute-start.9 = (f32[2,128,128]{2,1,0:T(8,128)S(1)}, f32[2,128,128]{2,1,0:T(8,128)S(1)}, u32[]{:S(2)}, u32[]{:S(2)}) collective-permute-start(f32[2,128,128]{2,1,0:T(8,128)S(1)} %multiply_add_fusion.2), channel_id=1, source_target_pairs={{128,0},{144,16},{160,32},{176,48},{192,64},{208,80},{224,96},{240... | collective-permute-start | bytes 393224 | tf_op jit(solution)/shard_map/ppermute | solution.py:15
  89.6 34.7 %all-to-all-start.1 = ((bf16[16,64,256]{2,1,0:T(8,128)(2,1)}), bf16[16,64,256]{2,1,0:T(8,128)(2,1)}, u32[]{:S(2)}, u32[]{:S(2)}) async-start(bf16[16,64,256]{2,1,0:T(8,128)(2,1)} %all_to_all.60), calls=%async_computation.1 | async-start | bytes 1048576 | tf_op jit(solution)/shard_map/all_to_all | solution.py:119
  99.1 10.5 %collective-permute-start.11 = (f32[2,128,128]{2,1,0:T(8,128)}, f32[2,128,128]{2,1,0:T(8,128)S(1)}, u32[]{:S(2)}, u32[]{:S(2)}) collective-permute-start(f32[2,128,128]{2,1,0:T(8,128)} %multiply_add_fusion.1), channel_id=1, source_target_pairs={{272,0},{288,16},{304,32},{320,48},{336,64},{352,80},{368,96},{384... | collective-permute-start | bytes 393224 | tf_op jit(solution)/shard_map/ppermute | solution.py:15
  106.4 9.5 %collective-permute-start.10 = (f32[2,128,128]{2,1,0:T(8,128)}, f32[2,128,128]{2,1,0:T(8,128)S(1)}, u32[]{:S(2)}, u32[]{:S(2)}) collective-permute-start(f32[2,128,128]{2,1,0:T(8,128)} %multiply_add_fusion.1), channel_id=1, source_target_pairs={{16,0},{32,16},{48,32},{64,48},{80,64},{96,80},{112,96},{128,112},... | collective-permute-start | bytes 393224 | tf_op jit(solution)/shard_map/ppermute | solution.py:15
  124.3 25.2 %all-to-all-start.2 = ((bf16[16,64,256]{2,1,0:T(8,128)(2,1)}), bf16[16,64,256]{2,1,0:T(8,128)(2,1)}, u32[]{:S(2)}, u32[]{:S(2)}) async-start(bf16[16,64,256]{2,1,0:T(8,128)(2,1)} %all_to_all.64), calls=%async_computation.2 | async-start | bytes 1048576 | tf_op jit(solution)/shard_map/all_to_all | solution.py:119
  149.6 20.3 %all-to-all-start = ((bf16[16,64,256]{2,1,0:T(8,128)(2,1)}), bf16[16,64,256]{2,1,0:T(8,128)(2,1)}, u32[]{:S(2)}, u32[]{:S(2)}) async-start(bf16[16,64,256]{2,1,0:T(8,128)(2,1)} %all_to_all.56), calls=%async_computation | async-start | bytes 1048576 | tf_op jit(solution)/shard_map/all_to_all | solution.py:119
  169.9 20.2 %all-to-all-start.3 = ((bf16[16,64,256]{2,1,0:T(8,128)(2,1)}), bf16[16,64,256]{2,1,0:T(8,128)(2,1)S(1)}, u32[]{:S(2)}, u32[]{:S(2)}) async-start(bf16[16,64,256]{2,1,0:T(8,128)(2,1)} %all_to_all.68), calls=%async_computation.3 | async-start | bytes 1048576 | tf_op jit(solution)/shard_map/all_to_all | solution.py:119
  (8 other events, 11.2 us)

commit v2 on v1

--- a/solution.py
+++ b/solution.py
@@ -1,35 +1,112 @@
+import functools
+
 import jax
 import jax.numpy as jnp
 from jax import lax
+from jax.experimental import pallas as pl
+from jax.experimental.pallas import tpu as pltpu
 from jax.sharding import PartitionSpec as P
 
 
-def decayed_scan(part, rate_len, axis, reverse):
-    count = lax.axis_size(axis)
-    place = lax.axis_index(axis)
-    ahead = count - 1 - place if reverse else place
-    sign = -1 if reverse else 1
-
-    def shifted(x, d):
-        pairs = [(s, s + sign * d) for s in range(count) if 0 <= s + sign * d < count]
-        return lax.ppermute(x, axis, pairs)
-
-    def weight(d):
-        return jnp.exp(-rate_len * d)[:, None, None]
-
-    total = part
+MESH = pl.DeviceIdType.MESH
+
+
+def scan_kernel(n, near, far, w_ref, k_ref, q_ref, s_out, r_out, kx, qx, krecv, qrecv, sems):
+    me = lax.axis_index("seq")
+    ex = lax.axis_index("exp")
+    heads = k_ref.shape[0]
+    barrier = pltpu.get_barrier_semaphore()
+    partners = sorted(set(near + [1, far]))
+    for d in partners:
+        for other in (me + d, me - d):
+            @pl.when(jnp.logical_and(other >= 0, other < n))
+            def _():
+                pl.semaphore_signal(barrier, 1, device_id=(other, ex), device_id_type=MESH)
+    peers = 0
+    for d in partners:
+        for other in (me + d, me - d):
+            peers = peers + jnp.logical_and(other >= 0, other < n).astype(jnp.int32)
+    pl.semaphore_wait(barrier, peers)
+
+    def copy(src, dst, slot, other):
+        return pltpu.make_async_remote_copy(
+            src_ref=src, dst_ref=dst, send_sem=sems.at[0, slot], recv_sem=sems.at[1, slot],
+            device_id=(lax.rem(other + n, n), ex), device_id_type=MESH,
+        )
+
+    sent = []
+    kcur, qcur = k_ref, q_ref
+    for r, d in enumerate(near):
+        kc = copy(kcur, krecv.at[r], 2 * r, me + d)
+        qc = copy(qcur, qrecv.at[r], 2 * r + 1, me - d)
+        pl.when(me + d < n)(kc.start)
+        pl.when(me - d >= 0)(qc.start)
+        sent.append((kc, me + d < n))
+        sent.append((qc, me - d >= 0))
+        for cur, nxt, recv, cp, has in ((kcur, kx, krecv, kc, me - d >= 0), (qcur, qx, qrecv, qc, me + d < n)):
+            @pl.when(has)
+            def _():
+                cp.wait_recv()
+                for h in range(heads):
+                    nxt[r, h] = cur[h] + w_ref[r * heads + h] * recv[r, h]
+
+            @pl.when(jnp.logical_not(has))
+            def _():
+                nxt[r] = cur[...]
+        kcur, qcur = kx.at[r], qx.at[r]
+    last = len(near)
+    finals = []
+    for j, d in enumerate((1, far)):
+        slot = 2 * (last + j)
+        kc = copy(kcur, krecv.at[last + j], slot, me + d)
+        qc = copy(qcur, qrecv.at[last + j], slot + 1, me - d)
+        pl.when(me + d < n)(kc.start)
+        pl.when(me - d >= 0)(qc.start)
+        sent.append((kc, me + d < n))
+        sent.append((qc, me - d >= 0))
+        finals.append((kc, qc, d))
+    s_out[...] = jnp.zeros_like(s_out)
+    r_out[...] = jnp.zeros_like(r_out)
+    for j, (kc, qc, d) in enumerate(finals):
+        for cp, recv, out, has in ((kc, krecv, s_out, me - d >= 0), (qc, qrecv, r_out, me + d < n)):
+            @pl.when(has)
+            def _():
+                cp.wait_recv()
+                for h in range(heads):
+                    scale = 1.0 if j == 0 else w_ref[last * heads + h]
+                    out[h] = out[h] + scale * recv[last + j, h]
+    for cp, cond in sent:
+        pl.when(cond)(cp.wait_send)
+
+
+def state_scan(dev_key, dev_query, rate_len, n):
+    near = []
     d = 1
-    while 2 * d < count:
-        got = shifted(total, d)
-        total = total + jnp.where(ahead >= d, weight(d), 0.0) * got
+    while 2 * d < n:
+        near.append(d)
         d *= 2
-    near = shifted(total, 1)
-    far_d = d + 1
-    result = jnp.where(ahead >= 1, 1.0, 0.0) * near
-    if far_d < count:
-        far = shifted(total, far_d)
-        result = result + jnp.where(ahead >= far_d, weight(d), 0.0) * far
-    return result
+    far = d + 1
+    heads = dev_key.shape[0]
+    dists = jnp.asarray(near + [d], jnp.float32)
+    weights = jnp.exp(-dists[:, None] * rate_len[None, :]).reshape(-1)
+    nrecv = len(near) + 2
+    body = functools.partial(scan_kernel, n, near, far)
+    state = jax.ShapeDtypeStruct(dev_key.shape, jnp.float32)
+    vspec = pl.BlockSpec(memory_space=pltpu.VMEM)
+    return pl.pallas_call(
+        body,
+        out_shape=(state, state),
+        in_specs=[pl.BlockSpec(memory_space=pltpu.SMEM), vspec, vspec],
+        out_specs=(vspec, vspec),
+        scratch_shapes=[
+            pltpu.VMEM((len(near),) + dev_key.shape, jnp.float32),
+            pltpu.VMEM((len(near),) + dev_key.shape, jnp.float32),
+            pltpu.VMEM((nrecv,) + dev_key.shape, jnp.float32),
+            pltpu.VMEM((nrecv,) + dev_key.shape, jnp.float32),
+            pltpu.SemaphoreType.DMA((2, 2 * nrecv)),
+        ],
+        compiler_params=pltpu.CompilerParams(collective_id=0, has_side_effects=True),
+    )(weights, dev_key, dev_query)
 
 
 def shards(query_tok, key_tok, value_tok, grad_out, decay_rate):
@@ -56,8 +133,7 @@
         "ihd,ihe->hde", query_product, upstream, preferred_element_type=jnp.float32
     )
     rate_len = decay_rate * seg_len
-    incoming = decayed_scan(dev_key, rate_len, "seq", False)
-    outgoing = decayed_scan(dev_query, rate_len, "seq", True)
+    incoming, outgoing = state_scan(dev_key, dev_query, rate_len, lax.axis_size("seq"))
     offsets = position[:, None] - position[None, :]
     over_rows = (((0,), (0,)), ((), ()))
     over_cols = (((1,), (1,)), ((), ()))

time: 192 us -> 173 us (0.901)
  the two profiles are of different devices: /device:TPU:7 before, /device:TPU:1 now
where the time goes in v2:
time: 173 us; the launch traced here: 172 us
  Pallas kernels  51.2 us (30%)
  waiting for transfers between devices  39.2 us (23%)
  matrix products  33.3 us (19%)
  local copies, waits for them, and re-layouts  23.3 us (13%)
  starting transfers between devices  21 us (12%)
  between operations  2.26 us (1%)
  other arithmetic  2.16 us (1%)
    pallas_call x1, Pallas kernels, state_scan(): pl.pallas_call(body, out_shape=(state, state), in_specs=[pl.BlockSpec(mem...  51.2 us
    all_to_all x4, waiting for transfers between devices, shards(): lax.all_to_all(results, 'exp', split_axis=0, concat_axis=1, tiled=True)  39.2 us
    all_to_all x4, starting transfers between devices, shards(): lax.all_to_all(results, 'exp', split_axis=0, concat_axis=1, tiled=True)  21 us
    all_to_all x8, local copies, waits for them, and re-layouts, shards(): lax.all_to_all(results, 'exp', split_axis=0, concat_axis=1, tiled=True)  10.9 us
    unnamed x26, local copies, waits for them, and re-layouts  6.91 us
    dot_general x2, matrix products, head_work(): lax.dot_general(query_one, key_one, over_cols, preferred_element_type=jnp...  6.18 us
    dot_general x2, matrix products, head_work(): lax.dot_general(upstream_one, value_one, over_cols, preferred_element_typ...  5.54 us
    dot_general x2, matrix products, head_work(): jnp.dot(gweights, key_one, preferred_element_type=jnp.float32)  4.6 us
  transfers between devices with their start and end apart: 4, of which 4 were waited for; matrix products, arithmetic and copies ran while one was open for 13% of the time, Pallas kernels for 0%

profile of v2, /device:TPU:1, one launch (start us, length us, event | category | flops | bytes accessed | tf_op | source)
XLA Modules:
  0.0 172.2 jit_solution(2027434877488917137)
XLA Ops:
  8.3 3.4 %multiply_convert_fusion = bf16[1024,1024]{1,0:T(8,128)(2,1)} fusion(f32[]{:T(128)} %bitcast.15, f32[]{:T(128)} %bitcast.14, bf16[1024,2,128]{0,2,1:T(8,128)(2,1)S(1)} %bitcast.215, bf16[1024,2,128]{0,2,1:T(8,128)(2,1)S(1)} %bitcast.194), kind=kOutput, calls=%fused_computation | convolution fusion | flops 276824064 | bytes 2621448 | tf_op jit(solution)/shard_map/dot_general | solution.py:153
  11.7 2.1 %multiply_convert_fusion.1 = bf16[1024,1024]{1,0:T(8,128)(2,1)S(1)} fusion(f32[]{:T(128)} %bitcast.5, f32[]{:T(128)} %bitcast.4, bf16[1024,2,128]{0,2,1:T(8,128)(2,1)S(1)} %bitcast.216, bf16[1024,2,128]{0,2,1:T(8,128)(2,1)S(1)} %bitcast.195), kind=kOutput, calls=%fused_computation.1 | convolution fusion | flops 276824064 | bytes 2621448 | tf_op jit(solution)/shard_map/dot_general | solution.py:153
  15.8 2.0 %copy.38 = bf16[1024,256]{0,1:T(8,128)(2,1)} copy(bf16[1024,256]{1,0:T(8,128)(2,1)} %param.7) | data formatting | bytes 1048576 | tf_op args[1]
  17.9 2.2 %fusion.34.k_ref = f32[2,128,128]{2,1,0:T(8,128)} fusion(bf16[1024,2,128]{0,2,1:T(8,128)(2,1)} %bitcast.217, bf16[1024,2,128]{0,2,1:T(8,128)(2,1)} %bitcast.208, f32[1024,2]{0,1:T(2,128)S(1)} %get-tuple-element.13), kind=kOutput, calls=%fused_computation.51 | convolution fusion | flops 67895296 | bytes 1187840 | tf_op jit(solution)/shard_map/ihd,ihe->hde/dot_general | solution.py:129
  20.2 3.1 %fusion.42 = f32[1024,128]{1,0:T(8,128)} fusion(bf16[1024,1024]{1,0:T(8,128)(2,1)} %multiply_convert_fusion, bf16[1024,2,128]{0,2,1:T(8,128)(2,1)} %bitcast.209), kind=kOutput, calls=%fused_computation.71 | convolution fusion | flops 268435456 | bytes 2883584 | tf_op jit(solution)/shard_map/dot_general | solution.py:163
  25.7 51.2 %shard_map.93 = (f32[2,128,128]{2,1,0:T(8,128)}, f32[2,128,128]{2,1,0:T(8,128)}) custom-call(f32[10]{0:T(128)} %exp.58.w_ref, f32[2,128,128]{2,1,0:T(8,128)} %fusion.34.k_ref, f32[2,128,128]{2,1,0:T(8,128)} %fusion.35.q_ref), custom_call_target="tpu_custom_call" | custom-call | tf_op jit(solution)/shard_map/pallas_call | solution.py:96
  76.9 1.6 fusion.30
  78.5 1.6 fusion.31
  81.4 2.2 %all_to_all.60 = bf16[16,64,256]{2,1,0:T(8,128)(2,1)} reshape(bf16[1024,2,128]{2,1,0:T(2,128)(2,1)} %copy.56) | data formatting | bytes 1048576 | tf_op jit(solution)/shard_map/all_to_all | solution.py:195
  83.6 9.7 %all-to-all-start.1 = ((bf16[16,64,256]{2,1,0:T(8,128)(2,1)}), bf16[16,64,256]{2,1,0:T(8,128)(2,1)}, u32[]{:S(2)}, u32[]{:S(2)}) async-start(bf16[16,64,256]{2,1,0:T(8,128)(2,1)} %all_to_all.60), calls=%async_computation.1 | async-start | bytes 1048576 | tf_op jit(solution)/shard_map/all_to_all | solution.py:195
  93.2 2.3 %fusion.41 = f32[1024,128]{1,0:T(8,128)S(1)} fusion(bf16[1024,1024]{1,0:T(8,128)(2,1)} %multiply_convert_fusion, bf16[1024,2,128]{0,2,1:T(8,128)(2,1)S(1)} %bitcast.202), kind=kOutput, calls=%fused_computation.70 | convolution fusion | flops 268435456 | bytes 2883584 | tf_op jit(solution)/shard_map/dot_general | solution.py:167
  99.3 3.1 %multiply_convert_fusion.2 = bf16[1024,1024]{1,0:T(8,128)(2,1)S(1)} fusion(f32[]{:T(128)} %bitcast.15, f32[]{:T(128)} %bitcast.14, bf16[1024,2,128]{0,2,1:T(8,128)(2,1)S(1)} %bitcast.204, bf16[1024,2,128]{0,2,1:T(8,128)(2,1)} %bitcast.210), kind=kOutput, calls=%fused_computation.2 | convolution fusion | flops 276824064 | bytes 2622464 | tf_op jit(solution)/shard_map/dot_general | solution.py:151
  102.5 1.5 fusion.43
  104.0 6.7 %all-to-all-done.1 = bf16[16,64,256]{2,1,0:T(8,128)(2,1)} async-done(((bf16[16,64,256]{2,1,0:T(8,128)(2,1)}), bf16[16,64,256]{2,1,0:T(8,128)(2,1)}, u32[]{:S(2)}, u32[]{:S(2)}) %all-to-all-start.1) | async-done | bytes 524320 | tf_op jit(solution)/shard_map/all_to_all | solution.py:195
  110.7 4.1 %all-to-all-start.2 = ((bf16[16,64,256]{2,1,0:T(8,128)(2,1)}), bf16[16,64,256]{2,1,0:T(8,128)(2,1)}, u32[]{:S(2)}, u32[]{:S(2)}) async-start(bf16[16,64,256]{2,1,0:T(8,128)(2,1)} %all_to_all.64), calls=%async_computation.2 | async-start | bytes 1048576 | tf_op jit(solution)/shard_map/all_to_all | solution.py:195
  114.8 1.5 fusion.32
  116.4 3.1 %multiply_convert_fusion.3 = bf16[1024,1024]{1,0:T(8,128)(2,1)S(1)} fusion(f32[]{:T(128)} %bitcast.5, f32[]{:T(128)} %bitcast.4, bf16[1024,2,128]{0,2,1:T(8,128)(2,1)S(1)} %bitcast.206, bf16[1024,2,128]{0,2,1:T(8,128)(2,1)} %bitcast.211), kind=kOutput, calls=%fused_computation.4 | convolution fusion | flops 276824064 | bytes 2622464 | tf_op jit(solution)/shard_map/dot_general | solution.py:151
  122.5 8.5 %all-to-all-done.2 = bf16[16,64,256]{2,1,0:T(8,128)(2,1)} async-done(((bf16[16,64,256]{2,1,0:T(8,128)(2,1)}), bf16[16,64,256]{2,1,0:T(8,128)(2,1)}, u32[]{:S(2)}, u32[]{:S(2)}) %all-to-all-start.2) | async-done | bytes 524320 | tf_op jit(solution)/shard_map/all_to_all | solution.py:195
  131.0 3.7 %all-to-all-start = ((bf16[16,64,256]{2,1,0:T(8,128)(2,1)}), bf16[16,64,256]{2,1,0:T(8,128)(2,1)S(1)}, u32[]{:S(2)}, u32[]{:S(2)}) async-start(bf16[16,64,256]{2,1,0:T(8,128)(2,1)} %all_to_all.56), calls=%async_computation | async-start | bytes 1048576 | tf_op jit(solution)/shard_map/all_to_all | solution.py:195
  139.4 11.8 %all-to-all-done = bf16[16,64,256]{2,1,0:T(8,128)(2,1)S(1)} async-done(((bf16[16,64,256]{2,1,0:T(8,128)(2,1)}), bf16[16,64,256]{2,1,0:T(8,128)(2,1)S(1)}, u32[]{:S(2)}, u32[]{:S(2)}) %all-to-all-start) | async-done | bytes 524320 | tf_op jit(solution)/shard_map/all_to_all | solution.py:195
  151.2 3.5 %all-to-all-start.3 = ((bf16[16,64,256]{2,1,0:T(8,128)(2,1)}), bf16[16,64,256]{2,1,0:T(8,128)(2,1)S(1)}, u32[]{:S(2)}, u32[]{:S(2)}) async-start(bf16[16,64,256]{2,1,0:T(8,128)(2,1)} %all_to_all.68), calls=%async_computation.3 | async-start | bytes 1048576 | tf_op jit(solution)/shard_map/all_to_all | solution.py:195
  154.7 1.9 %copy.77 = bf16[16,8,8,256]{3,2,0,1:T(8,128)(2,1)} copy(bf16[16,8,8,256]{3,2,1,0:T(8,128)(2,1)} %bitcast.66) | data formatting | bytes 1048576 | tf_op jit(solution)/shard_map/all_to_all | solution.py:195
  156.6 1.9 %copy.78 = bf16[16,8,8,256]{3,2,0,1:T(8,128)(2,1)} copy(bf16[16,8,8,256]{3,2,1,0:T(8,128)(2,1)} %bitcast.68) | data formatting | bytes 1048576 | tf_op jit(solution)/shard_map/all_to_all | solution.py:195
  159.3 12.1 %all-to-all-done.3 = bf16[16,64,256]{2,1,0:T(8,128)(2,1)S(1)} async-done(((bf16[16,64,256]{2,1,0:T(8,128)(2,1)}), bf16[16,64,256]{2,1,0:T(8,128)(2,1)S(1)}, u32[]{:S(2)}, u32[]{:S(2)}) %all-to-all-start.3) | async-done | bytes 524320 | tf_op jit(solution)/shard_map/all_to_all | solution.py:195
  (58 shorter events, 25.3 us)
Async XLA Ops:
  5.7 6.0 %copy-start.4 = (bf16[1024,256]{0,1:T(8,128)(2,1)}, bf16[1024,256]{0,1:T(8,128)(2,1)S(1)}, u32[]{:S(2)}) copy-start(bf16[1024,256]{0,1:T(8,128)(2,1)S(1)} %copy.40) | copy-start | bytes 1572868
  11.7 2.1 %copy-start.10 = (f32[5]{0:T(128)S(1)}, f32[5]{0:T(128)}, u32[]{:S(2)}) copy-start(f32[5]{0:T(128)} %constant.21) | copy-start | bytes 64
  17.8 5.4 %copy-start.2 = (bf16[1024,256]{0,1:T(8,128)(2,1)S(1)}, bf16[1024,256]{0,1:T(8,128)(2,1)}, u32[]{:S(2)}) copy-start(bf16[1024,256]{0,1:T(8,128)(2,1)} %copy.38) | copy-start | bytes 1572868
  83.6 27.1 %all-to-all-start.1 = ((bf16[16,64,256]{2,1,0:T(8,128)(2,1)}), bf16[16,64,256]{2,1,0:T(8,128)(2,1)}, u32[]{:S(2)}, u32[]{:S(2)}) async-start(bf16[16,64,256]{2,1,0:T(8,128)(2,1)} %all_to_all.60), calls=%async_computation.1 | async-start | bytes 1048576 | tf_op jit(solution)/shard_map/all_to_all | solution.py:195
  95.6 1.0 copy-start.5
  95.6 1.1 copy-start.8
  99.3 3.1 %copy-start.6 = (bf16[1024,256]{0,1:T(8,128)(2,1)S(1)}, bf16[1024,256]{0,1:T(8,128)(2,1)}, u32[]{:S(2)}) copy-start(bf16[1024,256]{0,1:T(8,128)(2,1)} %copy-done.4) | copy-start | bytes 1572868
  102.4 12.4 %copy-start.9 = (f32[2,128,128]{2,1,0:T(8,128)S(1)}, f32[2,128,128]{2,1,0:T(8,128)}, u32[]{:S(2)}) copy-start(f32[2,128,128]{2,1,0:T(8,128)} %get-tuple-element.6) | copy-start | bytes 393220
  110.7 20.3 %all-to-all-start.2 = ((bf16[16,64,256]{2,1,0:T(8,128)(2,1)}), bf16[16,64,256]{2,1,0:T(8,128)(2,1)}, u32[]{:S(2)}, u32[]{:S(2)}) async-start(bf16[16,64,256]{2,1,0:T(8,128)(2,1)} %all_to_all.64), calls=%async_computation.2 | async-start | bytes 1048576 | tf_op jit(solution)/shard_map/all_to_all | solution.py:195
  116.3 3.1 %copy-start.7 = (bf16[1024,256]{0,1:T(8,128)(2,1)S(1)}, bf16[1024,256]{0,1:T(8,128)(2,1)}, u32[]{:S(2)}) copy-start(bf16[1024,256]{0,1:T(8,128)(2,1)} %copy-done.4) | copy-start | bytes 1572868
  119.5 1.3 copy-start
  131.0 20.2 %all-to-all-start = ((bf16[16,64,256]{2,1,0:T(8,128)(2,1)}), bf16[16,64,256]{2,1,0:T(8,128)(2,1)S(1)}, u32[]{:S(2)}, u32[]{:S(2)}) async-start(bf16[16,64,256]{2,1,0:T(8,128)(2,1)} %all_to_all.56), calls=%async_computation | async-start | bytes 1048576 | tf_op jit(solution)/shard_map/all_to_all | solution.py:195
  134.7 1.0 copy-start.3
  134.7 1.8 %copy-start.1 = (bf16[1024,1024]{1,0:T(8,128)(2,1)S(1)}, bf16[1024,1024]{1,0:T(8,128)(2,1)}, u32[]{:S(2)}) copy-start(bf16[1024,1024]{1,0:T(8,128)(2,1)} %copy-done) | copy-start | bytes 6291460
  151.2 20.2 %all-to-all-start.3 = ((bf16[16,64,256]{2,1,0:T(8,128)(2,1)}), bf16[16,64,256]{2,1,0:T(8,128)(2,1)S(1)}, u32[]{:S(2)}, u32[]{:S(2)}) async-start(bf16[16,64,256]{2,1,0:T(8,128)(2,1)} %all_to_all.68), calls=%async_computation.3 | async-start | bytes 1048576 | tf_op jit(solution)/shard_map/all_to_all | solution.py:195

commit v3 on v2

--- a/solution.py
+++ b/solution.py
@@ -109,11 +109,110 @@
     )(weights, dev_key, dev_query)
 
 
+def fused_kernel(scal_ref, q_ref, k_ref, v_ref, do_ref, s_ref, r_ref, o0, o1, o2, o3,
+                 stage, wts, gwts, send_sems, recv_sems, local_sems):
+    outs = (o0, o1, o2, o3)
+    seq = lax.axis_index("seq")
+    me = lax.axis_index("exp")
+    ne = lax.axis_size("exp")
+    length, width = q_ref.shape
+    heads = scal_ref.shape[0] // 2
+    hd = width // heads
+    slab = length // ne
+    blk = min(256, length)
+    nblk = length // blk
+    hi = lax.Precision.HIGHEST
+    f32 = jnp.float32
+
+    barrier = pltpu.get_barrier_semaphore()
+    for j in range(1, ne):
+        pl.semaphore_signal(barrier, 1, device_id=(seq, lax.rem(me + j, ne)), device_id_type=MESH)
+    pl.semaphore_wait(barrier, ne - 1)
+
+    def cols(h):
+        return pl.ds(h * hd, hd)
+
+    for h in range(heads):
+        rate = scal_ref[h]
+        scale = scal_ref[heads + h]
+        qh = q_ref[:, cols(h)]
+        kh = k_ref[:, cols(h)]
+        vh = v_ref[:, cols(h)]
+        dh = do_ref[:, cols(h)]
+        for b in range(nblk):
+            rows = pl.ds(b * blk, blk)
+            i = (lax.broadcasted_iota(jnp.int32, (blk, length), 0) + b * blk).astype(f32)
+            jj = lax.broadcasted_iota(jnp.int32, (blk, length), 1).astype(f32)
+            off = i - jj
+            damp = jnp.where(off >= 0, jnp.exp(-rate * jnp.maximum(off, 0.0)), 0.0) * scale
+            sc = lax.dot_general(qh[b * blk:(b + 1) * blk], kh, (((1,), (1,)), ((), ())), preferred_element_type=f32)
+            wts[h, rows, :] = (sc * damp).astype(jnp.bfloat16)
+            gs = lax.dot_general(dh[b * blk:(b + 1) * blk], vh, (((1,), (1,)), ((), ())), preferred_element_type=f32)
+            gwts[h, rows, :] = (gs * damp).astype(jnp.bfloat16)
+
+    def send(o):
+        for j in range(1, ne):
+            peer = lax.rem(me + j, ne)
+            pltpu.make_async_remote_copy(
+                src_ref=stage.at[o, pl.ds(pl.multiple_of(peer * slab, slab), slab), :],
+                dst_ref=outs[o].at[:, pl.ds(pl.multiple_of(me * width, width), width)],
+                send_sem=send_sems.at[o, j], recv_sem=recv_sems.at[o, j],
+                device_id=(seq, peer), device_id_type=MESH,
+            ).start()
+        pltpu.make_async_copy(
+            stage.at[o, pl.ds(pl.multiple_of(me * slab, slab), slab), :],
+            outs[o].at[:, pl.ds(pl.multiple_of(me * width, width), width)],
+            local_sems.at[o],
+        ).start()
+
+    def pos(b):
+        return (lax.broadcasted_iota(jnp.int32, (blk, 1), 0) + b * blk).astype(f32)
+
+    for o in range(4):
+        for h in range(heads):
+            rate = scal_ref[h]
+            scale = scal_ref[heads + h]
+            for b in range(nblk):
+                rows = pl.ds(b * blk, blk)
+                if o == 0:
+                    lead = scale * jnp.exp(-rate * pos(b))
+                    res = jnp.dot(wts[h, rows, :], v_ref[:, cols(h)], preferred_element_type=f32)
+                    res = res + lead * jnp.dot(q_ref[rows, cols(h)].astype(f32), s_ref[h], precision=hi, preferred_element_type=f32)
+                elif o == 1:
+                    lead = scale * jnp.exp(-rate * pos(b))
+                    res = jnp.dot(gwts[h, rows, :], k_ref[:, cols(h)], preferred_element_type=f32)
+                    res = res + lead * lax.dot_general(do_ref[rows, cols(h)].astype(f32), s_ref[h], (((1,), (1,)), ((), ())), precision=hi, preferred_element_type=f32)
+                elif o == 2:
+                    trail = scale * jnp.exp(-rate * (length - 1.0 - pos(b)))
+                    res = lax.dot_general(gwts[h, :, rows], q_ref[:, cols(h)], (((0,), (0,)), ((), ())), preferred_element_type=f32)
+                    res = res + trail * lax.dot_general(v_ref[rows, cols(h)].astype(f32), r_ref[h], (((1,), (1,)), ((), ())), precision=hi, preferred_element_type=f32)
+                else:
+                    trail = scale * jnp.exp(-rate * (length - 1.0 - pos(b)))
+                    res = lax.dot_general(wts[h, :, rows], do_ref[:, cols(h)], (((0,), (0,)), ((), ())), preferred_element_type=f32)
+                    res = res + trail * jnp.dot(k_ref[rows, cols(h)].astype(f32), r_ref[h], precision=hi, preferred_element_type=f32)
+                stage[o, rows, cols(h)] = res.astype(jnp.bfloat16)
+        send(o)
+
+    for o in range(4):
+        for j in range(1, ne):
+            cp = pltpu.make_async_remote_copy(
+                src_ref=stage.at[o, pl.ds(0, slab), :],
+                dst_ref=outs[o].at[:, pl.ds(0, width)],
+                send_sem=send_sems.at[o, j], recv_sem=recv_sems.at[o, j],
+                device_id=(seq, lax.rem(me + j, ne)), device_id_type=MESH,
+            )
+            cp.wait_send()
+            cp.wait_recv()
+        pltpu.make_async_copy(
+            stage.at[o, pl.ds(0, slab), :], outs[o].at[:, pl.ds(0, width)], local_sems.at[o]
+        ).wait()
+
+
 def shards(query_tok, key_tok, value_tok, grad_out, decay_rate):
-    greatest_precision = lax.Precision.HIGHEST
     seg_len = query_tok.shape[0]
     num_heads = decay_rate.shape[0]
     head_size = query_tok.shape[1] // num_heads
+    ne = lax.axis_size("exp")
     total_len = seg_len * lax.axis_size("seq")
     scale_head = jnp.sqrt((2.0 * decay_rate + 2.0 / total_len) / head_size)
     shape_three = (seg_len, num_heads, head_size)
@@ -134,65 +233,29 @@
     )
     rate_len = decay_rate * seg_len
     incoming, outgoing = state_scan(dev_key, dev_query, rate_len, lax.axis_size("seq"))
-    offsets = position[:, None] - position[None, :]
-    over_rows = (((0,), (0,)), ((), ()))
-    over_cols = (((1,), (1,)), ((), ()))
-
-    def head_work(index):
-        rate = decay_rate[index]
-        scale = scale_head[index]
-        query_one = query_heads[:, index, :]
-        key_one = key_heads[:, index, :]
-        value_one = value_heads[:, index, :]
-        upstream_one = upstream[:, index, :]
-        start_state = incoming[index]
-        end_state = outgoing[index]
-        damping = jnp.where(offsets >= 0, jnp.exp(-rate * jnp.maximum(offsets, 0.0)), 0.0) * scale
-        scores = lax.dot_general(query_one, key_one, over_cols, preferred_element_type=jnp.float32)
-        weights = (scores * damping).astype(jnp.bfloat16)
-        grad_scores = lax.dot_general(
-            upstream_one, value_one, over_cols, preferred_element_type=jnp.float32
-        )
-        gweights = (grad_scores * damping).astype(jnp.bfloat16)
-        leading_scale = (scale * jnp.exp(-rate * position))[:, None]
-        trailing_scale = (scale * jnp.exp(-rate * (seg_len - 1.0 - position)))[:, None]
-        attended = jnp.dot(weights, value_one, preferred_element_type=jnp.float32)
-        attended = attended + leading_scale * jnp.dot(
-            query_one.astype(jnp.float32), start_state, precision=greatest_precision
-        )
-        query_gradient = jnp.dot(gweights, key_one, preferred_element_type=jnp.float32)
-        query_gradient = query_gradient + leading_scale * lax.dot_general(
-            upstream_one.astype(jnp.float32), start_state, over_cols, precision=greatest_precision
-        )
-        key_gradient = lax.dot_general(
-            gweights, query_one, over_rows, preferred_element_type=jnp.float32
-        )
-        key_gradient = key_gradient + trailing_scale * lax.dot_general(
-            value_one.astype(jnp.float32), end_state, over_cols, precision=greatest_precision
-        )
-        value_gradient = lax.dot_general(
-            weights, upstream_one, over_rows, preferred_element_type=jnp.float32
-        )
-        value_gradient = value_gradient + trailing_scale * jnp.dot(
-            key_one.astype(jnp.float32), end_state, precision=greatest_precision
-        )
-        return (
-            attended.astype(jnp.bfloat16),
-            query_gradient.astype(jnp.bfloat16),
-            key_gradient.astype(jnp.bfloat16),
-            value_gradient.astype(jnp.bfloat16),
-        )
-
-    head_outputs = [head_work(index) for index in range(num_heads)]
-    results = tuple(
-        (
-            jnp.stack([single[member] for single in head_outputs], axis=1).reshape(
-                seg_len, num_heads * head_size
-            )
-            for member in range(4)
-        )
-    )
-    return lax.all_to_all(results, "exp", split_axis=0, concat_axis=1, tiled=True)
+    scalars = jnp.concatenate([decay_rate, scale_head]).astype(jnp.float32)
+    width = query_tok.shape[1]
+    slab = seg_len // ne
+    out = jax.ShapeDtypeStruct((slab, ne * width), jnp.bfloat16)
+    vspec = pl.BlockSpec(memory_space=pltpu.VMEM)
+    anyspec = pl.BlockSpec(memory_space=pl.ANY)
+    return pl.pallas_call(
+        fused_kernel,
+        out_shape=(out, out, out, out),
+        in_specs=[pl.BlockSpec(memory_space=pltpu.SMEM)] + [vspec] * 6,
+        out_specs=(anyspec, anyspec, anyspec, anyspec),
+        scratch_shapes=[
+            pltpu.VMEM((4, seg_len, width), jnp.bfloat16),
+            pltpu.VMEM((num_heads, seg_len, seg_len), jnp.bfloat16),
+            pltpu.VMEM((num_heads, seg_len, seg_len), jnp.bfloat16),
+            pltpu.SemaphoreType.DMA((4, ne)),
+            pltpu.SemaphoreType.DMA((4, ne)),
+            pltpu.SemaphoreType.DMA((4,)),
+        ],
+        compiler_params=pltpu.CompilerParams(
+            collective_id=1, has_side_effects=True, vmem_limit_bytes=48 * 1024 * 1024
+        ),
+    )(scalars, query_tok, key_tok, value_tok, grad_out, incoming, outgoing)
 
 
 def solution(mesh):

time: 173 us -> 127 us (0.73)
  Pallas kernels: 51.2 us -> 114 us
  waiting for transfers between devices: 39.2 us -> 0 us
  matrix products: 33.3 us -> 1.93 us
  starting transfers between devices: 21 us -> 0 us
  local copies, waits for them, and re-layouts: 23.3 us -> 9.23 us
    pallas_call x0 -> x1, Pallas kernels: none -> 62.5 us  [shards(): pl.pallas_call(fused_kernel, out_shape=(out, out, out, out), in_specs=[pl...]
    all_to_all x4 -> x0, waiting for transfers between devices: 39.2 us -> none  [shards(): lax.all_to_all(results, 'exp', split_axis=0, concat_axis=1, tiled=True)]
    dot_general x20 -> x0, matrix products: 30.1 us -> none  [the longest x2 6.18 us: head_work(): lax.dot_general(query_one, key_one, over_cols, preferred_element_type=jnp...]
    all_to_all x4 -> x0, starting transfers between devices: 21 us -> none  [shards(): lax.all_to_all(results, 'exp', split_axis=0, concat_axis=1, tiled=True)]
    all_to_all x8 -> x0, local copies, waits for them, and re-layouts: 10.9 us -> none  [shards(): lax.all_to_all(results, 'exp', split_axis=0, concat_axis=1, tiled=True)]
    another operation x4 -> x0, local copies, waits for them, and re-layouts: 2.96 us -> none  [shards(): jnp.stack([single[member] for single in head_outputs], axis=1)]
    slice x2 -> x0, local copies, waits for them, and re-layouts: 1.87 us -> none  [the longest x1 1.31 us: head_work(): rate = decay_rate[index]]
    unnamed x26 -> x20, local copies, waits for them, and re-layouts: 6.91 us -> 7.13 us
  transfers between devices with their start and end apart: 4 -> 0, of which waited for: 4 -> 0; matrix products, arithmetic and copies ran while one was open for 13% -> 0% of each run, Pallas kernels for 0% -> 0%
where the time goes in v3:
time: 127 us; the launch traced here: 126 us
  Pallas kernels  114 us (90%)
  local copies, waits for them, and re-layouts  9.23 us (7%)
  matrix products  1.93 us (2%)
    pallas_call x1, Pallas kernels, shards(): pl.pallas_call(fused_kernel, out_shape=(out, out, out, out), in_specs=[pl...  62.5 us
    pallas_call x1, Pallas kernels, state_scan(): pl.pallas_call(body, out_shape=(state, state), in_specs=[pl.BlockSpec(mem...  51.2 us
    unnamed x20, local copies, waits for them, and re-layouts  7.13 us

profile of v3, /device:TPU:1, one launch (start us, length us, event | category | flops | bytes accessed | tf_op | source)
XLA Modules:
  0.0 126.5 jit_solution(14236461433684150189)
XLA Ops:
  0.6 0.7 fusion.8
  1.3 0.7 copy-done.7
  2.0 0.1 pad_maximum_fusion.scal_ref
  2.0 0.6 copy-done.6
  2.6 0.1 multiply_exponential_fusion.2
  2.7 0.6 exp.22.w_ref
  3.3 0.1 multiply_exponential_fusion
  3.4 0.0 copy-start.3
  3.4 1.3 %copy.19 = f32[1024,256]{0,1:T(8,128)S(1)} copy(bf16[1024,256]{1,0:T(8,128)(2,1)} %q_ref.1) | data formatting | bytes 1572864 | tf_op jit(solution)/shard_map/convert_element_type | solution.py:227
  4.7 0.0 copy-done.3
  4.7 0.0 copy-start.1
  4.7 1.0 fusion.1.q_ref
  5.7 0.1 copy-done.1
  5.8 0.2 copy.18
  6.0 0.8 copy-done.2
  6.8 1.0 fusion.k_ref
  7.8 51.2 %shard_map.93 = (f32[2,128,128]{2,1,0:T(8,128)}, f32[2,128,128]{2,1,0:T(8,128)}) custom-call(f32[10]{0:T(128)} %exp.22.w_ref, f32[2,128,128]{2,1,0:T(8,128)} %fusion.k_ref, f32[2,128,128]{2,1,0:T(8,128)} %fusion.1.q_ref), custom_call_target="tpu_custom_call" | custom-call | tf_op jit(solution)/shard_map/pallas_call | solution.py:96
  59.0 0.9 copy-done.4
  59.9 0.9 copy-done.5
  60.8 62.5 %shard_map.94 = (bf16[64,4096]{1,0:T(8,128)(2,1)S(1)}, bf16[64,4096]{1,0:T(8,128)(2,1)S(1)}, bf16[64,4096]{1,0:T(8,128)(2,1)S(1)}, bf16[64,4096]{1,0:T(8,128)(2,1)S(1)}) custom-call(f32[4]{0:T(128)S(1)} %pad_maximum_fusion.scal_ref, bf16[1024,256]{1,0:T(8,128)(2,1)S(1)} %copy-done, bf16[1024,256]{1,0:T(8,128)(2,1)S(1)} %copy-done.1, ...), custom_call_target="tpu_custom_call" | custom-call | tf_op jit(solution)/shard_map/pallas_call | solution.py:242
  123.3 0.8 copy.34
  124.1 0.8 copy.35
  124.9 0.8 copy.36
  125.7 0.8 copy.37
  (8 shorter events, 0.0 us)
Async XLA Ops:
  1.3 0.7 copy-start.7
  2.0 0.7 copy-start.6
  3.4 1.3 %copy-start.3 = (bf16[1024,256]{1,0:T(8,128)(2,1)S(1)}, bf16[1024,256]{1,0:T(8,128)(2,1)}, u32[]{:S(2)}) copy-start(bf16[1024,256]{1,0:T(8,128)(2,1)} %do_ref.1) | copy-start | bytes 1572868
  4.7 1.0 copy-start.1
  5.8 1.0 copy-start.2
  6.8 52.2 %copy-start = (bf16[1024,256]{1,0:T(8,128)(2,1)S(1)}, bf16[1024,256]{1,0:T(8,128)(2,1)}, u32[]{:S(2)}) copy-start(bf16[1024,256]{1,0:T(8,128)(2,1)} %q_ref.1) | copy-start | bytes 1572868
  59.0 0.9 copy-start.4
  59.9 0.9 copy-start.5

commit v4 on v3

v4 whole, which is shorter than its diff:
```python
import functools

import jax
import jax.numpy as jnp
from jax import lax
from jax.experimental import pallas as pl
from jax.experimental.pallas import tpu as pltpu
from jax.sharding import PartitionSpec as P


MESH = pl.DeviceIdType.MESH


def whole_kernel(n, near, far, w_ref, scal_ref, q_ref, k_ref, v_ref, do_ref, dk_ref, dq_ref,
                 o0, o1, o2, o3, kx, qx, krecv, qrecv, s_acc, r_acc, intra, stage, wts, gwts,
                 scan_sems, send_sems, recv_sems, local_sems):
    outs = (o0, o1, o2, o3)
    me_s = lax.axis_index("seq")
    me = lax.axis_index("exp")
    ne = lax.axis_size("exp")
    length, width = q_ref.shape
    heads = scal_ref.shape[0] // 2
    hd = width // heads
    slab = length // ne
    blk = min(256, length)
    nblk = length // blk
    hi = lax.Precision.HIGHEST
    f32 = jnp.float32
    nt = (((1,), (1,)), ((), ()))
    tn = (((0,), (0,)), ((), ()))

    barrier = pltpu.get_barrier_semaphore()
    partners = sorted(set(near + [1, far]))
    peers = ne - 1
    for d in partners:
        for other in (me_s + d, me_s - d):
            @pl.when(jnp.logical_and(other >= 0, other < n))
            def _():
                pl.semaphore_signal(barrier, 1, device_id=(other, me), device_id_type=MESH)
            peers = peers + jnp.logical_and(other >= 0, other < n).astype(jnp.int32)
    for j in range(1, ne):
        pl.semaphore_signal(barrier, 1, device_id=(me_s, lax.rem(me + j, ne)), device_id_type=MESH)
    pl.semaphore_wait(barrier, peers)

    def cols(h):
        return pl.ds(h * hd, hd)

    def weights_task(h):
        def run():
            rate = scal_ref[h]
            scale = scal_ref[heads + h]
            qh = q_ref[:, cols(h)]
            kh = k_ref[:, cols(h)]
            vh = v_ref[:, cols(h)]
            dh = do_ref[:, cols(h)]
            for b in range(nblk):
                rows = pl.ds(b * blk, blk)
                i = (lax.broadcasted_iota(jnp.int32, (blk, length), 0) + b * blk).astype(f32)
                jj = lax.broadcasted_iota(jnp.int32, (blk, length), 1).astype(f32)
                off = i - jj
                damp = jnp.where(off >= 0, jnp.exp(-rate * jnp.maximum(off, 0.0)), 0.0) * scale
                sc = lax.dot_general(qh[b * blk:(b + 1) * blk], kh, nt, preferred_element_type=f32)
                wts[h, rows, :] = (sc * damp).astype(jnp.bfloat16)
                gs = lax.dot_general(dh[b * blk:(b + 1) * blk], vh, nt, preferred_element_type=f32)
                gwts[h, rows, :] = (gs * damp).astype(jnp.bfloat16)
        return run

    def intra_task(h, o):
        def run():
            for b in range(nblk):
                rows = pl.ds(b * blk, blk)
                if o == 0:
                    res = jnp.dot(wts[h, rows, :], v_ref[:, cols(h)], preferred_element_type=f32)
                elif o == 1:
                    res = jnp.dot(gwts[h, rows, :], k_ref[:, cols(h)], preferred_element_type=f32)
                elif o == 2:
                    res = lax.dot_general(gwts[h, :, rows], q_ref[:, cols(h)], tn, preferred_element_type=f32)
                else:
                    res = lax.dot_general(wts[h, :, rows], do_ref[:, cols(h)], tn, preferred_element_type=f32)
                intra[o, rows, cols(h)] = res
        return run

    tasks = []
    for h in range(heads):
        tasks.append(weights_task(h))
        tasks.extend(intra_task(h, o) for o in range(4))

    def copy(src, dst, slot, other):
        return pltpu.make_async_remote_copy(
            src_ref=src, dst_ref=dst, send_sem=scan_sems.at[0, slot], recv_sem=scan_sems.at[1, slot],
            device_id=(lax.rem(other + n, n), me), device_id_type=MESH,
        )

    nround = len(near) + 1
    per_round = -(-len(tasks) // nround)
    sent = []
    kcur, qcur = dk_ref, dq_ref
    for r, d in enumerate(near):
        kc = copy(kcur, krecv.at[r], 2 * r, me_s + d)
        qc = copy(qcur, qrecv.at[r], 2 * r + 1, me_s - d)
        pl.when(me_s + d < n)(kc.start)
        pl.when(me_s - d >= 0)(qc.start)
        sent.append((kc, me_s + d < n))
        sent.append((qc, me_s - d >= 0))
        for task in tasks[r * per_round:(r + 1) * per_round]:
            task()
        for cur, nxt, recv, cp, has in ((kcur, kx, krecv, kc, me_s - d >= 0), (qcur, qx, qrecv, qc, me_s + d < n)):
            @pl.when(has)
            def _():
                cp.wait_recv()
                for h in range(heads):
                    nxt[r, h] = cur[h] + w_ref[r * heads + h] * recv[r, h]

            @pl.when(jnp.logical_not(has))
            def _():
                nxt[r] = cur[...]
        kcur, qcur = kx.at[r], qx.at[r]
    last = len(near)
    finals = []
    for j, d in enumerate((1, far)):
        slot = 2 * (last + j)
        kc = copy(kcur, krecv.at[last + j], slot, me_s + d)
        qc = copy(qcur, qrecv.at[last + j], slot + 1, me_s - d)
        pl.when(me_s + d < n)(kc.start)
        pl.when(me_s - d >= 0)(qc.start)
        sent.append((kc, me_s + d < n))
        sent.append((qc, me_s - d >= 0))
        finals.append((kc, qc, d))
    for task in tasks[last * per_round:]:
        task()
    s_acc[...] = jnp.zeros_like(s_acc)
    r_acc[...] = jnp.zeros_like(r_acc)
    for j, (kc, qc, d) in enumerate(finals):
        for cp, recv, acc, has in ((kc, krecv, s_acc, me_s - d >= 0), (qc, qrecv, r_acc, me_s + d < n)):
            @pl.when(has)
            def _():
                cp.wait_recv()
                for h in range(heads):
                    scale = 1.0 if j == 0 else w_ref[last * heads + h]
                    acc[h] = acc[h] + scale * recv[last + j, h]

    def send(o):
        for j in range(1, ne):
            peer = lax.rem(me + j, ne)
            pltpu.make_async_remote_copy(
                src_ref=stage.at[o, pl.ds(pl.multiple_of(peer * slab, slab), slab), :],
                dst_ref=outs[o].at[:, pl.ds(pl.multiple_of(me * width, width), width)],
                send_sem=send_sems.at[o, j], recv_sem=recv_sems.at[o, j],
                device_id=(me_s, peer), device_id_type=MESH,
            ).start()
        pltpu.make_async_copy(
            stage.at[o, pl.ds(pl.multiple_of(me * slab, slab), slab), :],
            outs[o].at[:, pl.ds(pl.multiple_of(me * width, width), width)],
            local_sems.at[o],
        ).start()

    def pos(b):
        return (lax.broadcasted_iota(jnp.int32, (blk, 1), 0) + b * blk).astype(f32)

    for o in range(4):
        for h in range(heads):
            rate = scal_ref[h]
            scale = scal_ref[heads + h]
            for b in range(nblk):
                rows = pl.ds(b * blk, blk)
                if o == 0:
                    lead = scale * jnp.exp(-rate * pos(b))
                    extra = lead * jnp.dot(q_ref[rows, cols(h)].astype(f32), s_acc[h], precision=hi, preferred_element_type=f32)
                elif o == 1:
                    lead = scale * jnp.exp(-rate * pos(b))
                    extra = lead * lax.dot_general(do_ref[rows, cols(h)].astype(f32), s_acc[h], nt, precision=hi, preferred_element_type=f32)
                elif o == 2:
                    trail = scale * jnp.exp(-rate * (length - 1.0 - pos(b)))
                    extra = trail * lax.dot_general(v_ref[rows, cols(h)].astype(f32), r_acc[h], nt, precision=hi, preferred_element_type=f32)
                else:
                    trail = scale * jnp.exp(-rate * (length - 1.0 - pos(b)))
                    extra = trail * jnp.dot(k_ref[rows, cols(h)].astype(f32), r_acc[h], precision=hi, preferred_element_type=f32)
                stage[o, rows, cols(h)] = (intra[o, rows, cols(h)] + extra).astype(jnp.bfloat16)
        send(o)

    for cp, cond in sent:
        pl.when(cond)(cp.wait_send)
    for o in range(4):
        for j in range(1, ne):
            cp = pltpu.make_async_remote_copy(
                src_ref=stage.at[o, pl.ds(0, slab), :],
                dst_ref=outs[o].at[:, pl.ds(0, width)],
                send_sem=send_sems.at[o, j], recv_sem=recv_sems.at[o, j],
                device_id=(me_s, lax.rem(me + j, ne)), device_id_type=MESH,
            )
            cp.wait_send()
            cp.wait_recv()
        pltpu.make_async_copy(
            stage.at[o, pl.ds(0, slab), :], outs[o].at[:, pl.ds(0, width)], local_sems.at[o]
        ).wait()


def shards(query_tok, key_tok, value_tok, grad_out, decay_rate):
    seg_len = query_tok.shape[0]
    num_heads = decay_rate.shape[0]
    head_size = query_tok.shape[1] // num_heads
    ne = lax.axis_size("exp")
    total_len = seg_len * lax.axis_size("seq")
    scale_head = jnp.sqrt((2.0 * decay_rate + 2.0 / total_len) / head_size)
    shape_three = (seg_len, num_heads, head_size)
    query_heads = query_tok.reshape(shape_three)
    key_heads = key_tok.reshape(shape_three)
    value_heads = value_tok.reshape(shape_three)
    upstream = grad_out.reshape(shape_three)
    position = jnp.arange(seg_len, dtype=jnp.float32)
    to_end = jnp.exp(-decay_rate[None, :] * (seg_len - position[:, None]))
    from_start = jnp.exp(-decay_rate[None, :] * (position[:, None] + 1.0))
    key_product = (key_heads * to_end[:, :, None]).astype(jnp.bfloat16)
    query_product = (query_heads * from_start[:, :, None]).astype(jnp.bfloat16)
    dev_key = jnp.einsum(
        "ihd,ihe->hde", key_product, value_heads, preferred_element_type=jnp.float32
    )
    dev_query = jnp.einsum(
        "ihd,ihe->hde", query_product, upstream, preferred_element_type=jnp.float32
    )
    rate_len = decay_rate * seg_len
    n = lax.axis_size("seq")
    near = []
    d = 1
    while 2 * d < n:
        near.append(d)
        d *= 2
    far = d + 1
    dists = jnp.asarray(near + [d], jnp.float32)
    weights = jnp.exp(-dists[:, None] * rate_len[None, :]).reshape(-1)
    nrecv = len(near) + 2
    scalars = jnp.concatenate([decay_rate, scale_head]).astype(jnp.float32)
    width = query_tok.shape[1]
    slab = seg_len // ne
    out = jax.ShapeDtypeStruct((slab, ne * width), jnp.bfloat16)
    smem = pl.BlockSpec(memory_space=pltpu.SMEM)
    vspec = pl.BlockSpec(memory_space=pltpu.VMEM)
    anyspec = pl.BlockSpec(memory_space=pl.ANY)
    st = dev_key.shape
    return pl.pallas_call(
        functools.partial(whole_kernel, n, near, far),
        out_shape=(out, out, out, out),
        in_specs=[smem, smem] + [vspec] * 6,
        out_specs=(anyspec, anyspec, anyspec, anyspec),
        scratch_shapes=[
            pltpu.VMEM((len(near),) + st, jnp.float32),
            pltpu.VMEM((len(near),) + st, jnp.float32),
            pltpu.VMEM((nrecv,) + st, jnp.float32),
            pltpu.VMEM((nrecv,) + st, jnp.float32),
            pltpu.VMEM(st, jnp.float32),
            pltpu.VMEM(st, jnp.float32),
            pltpu.VMEM((4, seg_len, width), jnp.float32),
            pltpu.VMEM((4, seg_len, width), jnp.bfloat16),
            pltpu.VMEM((num_heads, seg_len, seg_len), jnp.bfloat16),
            pltpu.VMEM((num_heads, seg_len, seg_len), jnp.bfloat16),
            pltpu.SemaphoreType.DMA((2, 2 * nrecv)),
            pltpu.SemaphoreType.DMA((4, ne)),
            pltpu.SemaphoreType.DMA((4, ne)),
            pltpu.SemaphoreType.DMA((4,)),
        ],
        compiler_params=pltpu.CompilerParams(
            collective_id=0, has_side_effects=True, vmem_limit_bytes=56 * 1024 * 1024
        ),
    )(weights, scalars, query_tok, key_tok, value_tok, grad_out, dev_key, dev_query)


def solution(mesh):
    placed = (P("seq", "exp"), P("seq", "exp"), P("seq", "exp"), P("seq", "exp"), P("exp"))
    return jax.shard_map(
        shards,
        mesh=mesh,
        in_specs=placed,
        out_specs=(
            P(("seq", "exp"), None),
            P(("seq", "exp"), None),
            P(("seq", "exp"), None),
            P(("seq", "exp"), None),
        ),
        check_vma=False,
    )
```

time: 127 us -> 118 us (0.929)
  the two profiles are of different devices: /device:TPU:1 before, /device:TPU:83 now
where the time goes in v4:
time: 118 us
  Pallas kernels  105 us (89%)
  local copies, waits for them, and re-layouts  8.93 us (8%)
  matrix products  1.91 us (2%)
  other arithmetic  1.42 us (1%)
    pallas_call x1, Pallas kernels, shards(): pl.pallas_call(functools.partial(whole_kernel, n, near, far), out_shape=(...  105 us
    unnamed x20, local copies, waits for them, and re-layouts  6.83 us

profile of v4, /device:TPU:83, one launch (start us, length us, event | category | flops | bytes accessed | tf_op | source)
XLA Modules:
  0.0 117.8 jit_solution(6336953496008505508)
XLA Ops:
  0.6 0.7 fusion.8
  1.3 0.7 copy-done.7
  2.0 0.6 pad_maximum_fusion.scal_ref
  2.5 0.1 copy-done.6
  2.6 0.1 multiply_exponential_fusion.2
  2.7 0.6 exp.22.w_ref
  3.3 0.1 multiply_exponential_fusion
  3.4 0.0 copy-start.2
  3.4 1.3 %copy.19 = f32[1024,256]{0,1:T(8,128)S(1)} copy(bf16[1024,256]{1,0:T(8,128)(2,1)} %q_ref.1) | data formatting | bytes 1572864 | tf_op jit(solution)/shard_map/convert_element_type | solution.py:214
  4.7 0.0 copy-done.2
  4.7 0.0 copy-start
  4.7 1.0 fusion.1.dq_ref
  5.7 0.1 copy-done
  5.8 0.2 copy.18
  6.0 0.8 copy-done.1
  6.8 1.0 fusion.dk_ref
  7.8 104.8 %shard_map.93 = (bf16[64,4096]{1,0:T(8,128)(2,1)}, bf16[64,4096]{1,0:T(8,128)(2,1)}, bf16[64,4096]{1,0:T(8,128)(2,1)}, bf16[64,4096]{1,0:T(8,128)(2,1)}) custom-call(f32[10]{0:T(128)} %exp.22.w_ref, f32[4]{0:T(128)} %pad_maximum_fusion.scal_ref, bf16[1024,256]{1,0:T(8,128)(2,1)} %q_ref.1, bf16[1024,256]{1,0:T(8,128)(2,1)} %k_ref.1, bf16[1024,256]{1,0:T(8,128)(2,1)} %v_ref.1, ...), custom_call_target="tpu_custom_call" | custom-call | tf_op jit(solution)/shard_map/pallas_call | solution.py:240
  112.6 0.0 copy-start.5
  112.6 1.9 %copy.34 = bf16[64,4096]{1,0:T(8,128)(2,1)} copy(bf16[64,4096]{1,0:T(8,128)(2,1)} %get-tuple-element.15) | data formatting | bytes 1048576
  114.5 0.8 copy.35
  115.3 0.4 copy-done.4
  115.7 0.8 copy.36
  116.5 0.4 copy-done.3
  117.0 0.8 copy.37
  (7 shorter events, 0.0 us)
Async XLA Ops:
  1.3 0.7 copy-start.7
  2.0 0.7 copy-start.6
  3.4 1.3 %copy-start.2 = (bf16[1024,256]{1,0:T(8,128)(2,1)S(1)}, bf16[1024,256]{1,0:T(8,128)(2,1)}, u32[]{:S(2)}) copy-start(bf16[1024,256]{1,0:T(8,128)(2,1)} %do_ref.1) | copy-start | bytes 1572868
  4.7 1.0 copy-start
  5.8 1.0 copy-start.1
  112.6 1.9 %copy-start.5 = (bf16[64,4096]{1,0:T(8,128)(2,1)S(1)}, bf16[64,4096]{1,0:T(8,128)(2,1)}, u32[]{:S(2)}) copy-start(bf16[64,4096]{1,0:T(8,128)(2,1)} %get-tuple-element.16) | copy-start | bytes 1572868
  114.5 1.2 %copy-start.4 = (bf16[64,4096]{1,0:T(8,128)(2,1)S(1)}, bf16[64,4096]{1,0:T(8,128)(2,1)}, u32[]{:S(2)}) copy-start(bf16[64,4096]{1,0:T(8,128)(2,1)} %get-tuple-element.17) | copy-start | bytes 1572868
  115.7 1.2 %copy-start.3 = (bf16[64,4096]{1,0:T(8,128)(2,1)S(1)}, bf16[64,4096]{1,0:T(8,128)(2,1)}, u32[]{:S(2)}) copy-start(bf16[64,4096]{1,0:T(8,128)(2,1)} %get-tuple-element.18) | copy-start | bytes 1572868

commit v5 on v4

--- a/solution.py
+++ b/solution.py
@@ -80,87 +80,81 @@
                 intra[o, rows, cols(h)] = res
         return run
 
-    tasks = []
-    for h in range(heads):
-        tasks.append(weights_task(h))
-        tasks.extend(intra_task(h, o) for o in range(4))
-
-    def copy(src, dst, slot, other):
+    def copy(src, dst, h, slot, other):
         return pltpu.make_async_remote_copy(
-            src_ref=src, dst_ref=dst, send_sem=scan_sems.at[0, slot], recv_sem=scan_sems.at[1, slot],
+            src_ref=src, dst_ref=dst, send_sem=scan_sems.at[0, h, slot], recv_sem=scan_sems.at[1, h, slot],
             device_id=(lax.rem(other + n, n), me), device_id_type=MESH,
         )
 
-    nround = len(near) + 1
-    per_round = -(-len(tasks) // nround)
-    sent = []
-    kcur, qcur = dk_ref, dq_ref
-    for r, d in enumerate(near):
-        kc = copy(kcur, krecv.at[r], 2 * r, me_s + d)
-        qc = copy(qcur, qrecv.at[r], 2 * r + 1, me_s - d)
-        pl.when(me_s + d < n)(kc.start)
-        pl.when(me_s - d >= 0)(qc.start)
-        sent.append((kc, me_s + d < n))
-        sent.append((qc, me_s - d >= 0))
-        for task in tasks[r * per_round:(r + 1) * per_round]:
-            task()
-        for cur, nxt, recv, cp, has in ((kcur, kx, krecv, kc, me_s - d >= 0), (qcur, qx, qrecv, qc, me_s + d < n)):
-            @pl.when(has)
-            def _():
-                cp.wait_recv()
-                for h in range(heads):
-                    nxt[r, h] = cur[h] + w_ref[r * heads + h] * recv[r, h]
-
-            @pl.when(jnp.logical_not(has))
-            def _():
-                nxt[r] = cur[...]
-        kcur, qcur = kx.at[r], qx.at[r]
-    last = len(near)
-    finals = []
-    for j, d in enumerate((1, far)):
-        slot = 2 * (last + j)
-        kc = copy(kcur, krecv.at[last + j], slot, me_s + d)
-        qc = copy(qcur, qrecv.at[last + j], slot + 1, me_s - d)
-        pl.when(me_s + d < n)(kc.start)
-        pl.when(me_s - d >= 0)(qc.start)
-        sent.append((kc, me_s + d < n))
-        sent.append((qc, me_s - d >= 0))
-        finals.append((kc, qc, d))
-    for task in tasks[last * per_round:]:
-        task()
-    s_acc[...] = jnp.zeros_like(s_acc)
-    r_acc[...] = jnp.zeros_like(r_acc)
-    for j, (kc, qc, d) in enumerate(finals):
-        for cp, recv, acc, has in ((kc, krecv, s_acc, me_s - d >= 0), (qc, qrecv, r_acc, me_s + d < n)):
-            @pl.when(has)
-            def _():
-                cp.wait_recv()
-                for h in range(heads):
-                    scale = 1.0 if j == 0 else w_ref[last * heads + h]
-                    acc[h] = acc[h] + scale * recv[last + j, h]
-
-    def send(o):
+    def send(o, h):
         for j in range(1, ne):
             peer = lax.rem(me + j, ne)
             pltpu.make_async_remote_copy(
-                src_ref=stage.at[o, pl.ds(pl.multiple_of(peer * slab, slab), slab), :],
-                dst_ref=outs[o].at[:, pl.ds(pl.multiple_of(me * width, width), width)],
-                send_sem=send_sems.at[o, j], recv_sem=recv_sems.at[o, j],
+                src_ref=stage.at[o, pl.ds(pl.multiple_of(peer * slab, slab), slab), cols(h)],
+                dst_ref=outs[o].at[:, pl.ds(pl.multiple_of(me * width + h * hd, hd), hd)],
+                send_sem=send_sems.at[o, h, j], recv_sem=recv_sems.at[o, h, j],
                 device_id=(me_s, peer), device_id_type=MESH,
             ).start()
         pltpu.make_async_copy(
-            stage.at[o, pl.ds(pl.multiple_of(me * slab, slab), slab), :],
-            outs[o].at[:, pl.ds(pl.multiple_of(me * width, width), width)],
-            local_sems.at[o],
+            stage.at[o, pl.ds(pl.multiple_of(me * slab, slab), slab), cols(h)],
+            outs[o].at[:, pl.ds(pl.multiple_of(me * width + h * hd, hd), hd)],
+            local_sems.at[o, h],
         ).start()
 
     def pos(b):
         return (lax.broadcasted_iota(jnp.int32, (blk, 1), 0) + b * blk).astype(f32)
 
-    for o in range(4):
-        for h in range(heads):
-            rate = scal_ref[h]
-            scale = scal_ref[heads + h]
+    nround = len(near) + 1
+    sent = []
+    last = len(near)
+    for h in range(heads):
+        mine = [weights_task(h)] + [intra_task(h, o) for o in range(4)]
+        per_round = -(-len(mine) // nround)
+        kcur, qcur = dk_ref.at[h], dq_ref.at[h]
+        for r, d in enumerate(near):
+            kc = copy(kcur, krecv.at[r, h], h, 2 * r, me_s + d)
+            qc = copy(qcur, qrecv.at[r, h], h, 2 * r + 1, me_s - d)
+            pl.when(me_s + d < n)(kc.start)
+            pl.when(me_s - d >= 0)(qc.start)
+            sent.append((kc, me_s + d < n))
+            sent.append((qc, me_s - d >= 0))
+            for task in mine[r * per_round:(r + 1) * per_round]:
+                task()
+            for cur, nxt, recv, cp, has in ((kcur, kx, krecv, kc, me_s - d >= 0), (qcur, qx, qrecv, qc, me_s + d < n)):
+                @pl.when(has)
+                def _():
+                    cp.wait_recv()
+                    nxt[r, h] = cur[...] + w_ref[r * heads + h] * recv[r, h]
+
+                @pl.when(jnp.logical_not(has))
+                def _():
+                    nxt[r, h] = cur[...]
+            kcur, qcur = kx.at[r, h], qx.at[r, h]
+        finals = []
+        for j, d in enumerate((1, far)):
+            slot = 2 * (last + j)
+            kc = copy(kcur, krecv.at[last + j, h], h, slot, me_s + d)
+            qc = copy(qcur, qrecv.at[last + j, h], h, slot + 1, me_s - d)
+            pl.when(me_s + d < n)(kc.start)
+            pl.when(me_s - d >= 0)(qc.start)
+            sent.append((kc, me_s + d < n))
+            sent.append((qc, me_s - d >= 0))
+            finals.append((kc, qc, d))
+        for task in mine[last * per_round:]:
+            task()
+        s_acc[h] = jnp.zeros((hd, hd), f32)
+        r_acc[h] = jnp.zeros((hd, hd), f32)
+        for j, (kc, qc, d) in enumerate(finals):
+            for cp, recv, acc, has in ((kc, krecv, s_acc, me_s - d >= 0), (qc, qrecv, r_acc, me_s + d < n)):
+                @pl.when(has)
+                def _():
+                    cp.wait_recv()
+                    scale = 1.0 if j == 0 else w_ref[last * heads + h]
+                    acc[h] = acc[h] + scale * recv[last + j, h]
+
+        rate = scal_ref[h]
+        scale = scal_ref[heads + h]
+        for o in range(4):
             for b in range(nblk):
                 rows = pl.ds(b * blk, blk)
                 if o == 0:
@@ -176,23 +170,24 @@
                     trail = scale * jnp.exp(-rate * (length - 1.0 - pos(b)))
                     extra = trail * jnp.dot(k_ref[rows, cols(h)].astype(f32), r_acc[h], precision=hi, preferred_element_type=f32)
                 stage[o, rows, cols(h)] = (intra[o, rows, cols(h)] + extra).astype(jnp.bfloat16)
-        send(o)
+            send(o, h)
 
     for cp, cond in sent:
         pl.when(cond)(cp.wait_send)
     for o in range(4):
-        for j in range(1, ne):
-            cp = pltpu.make_async_remote_copy(
-                src_ref=stage.at[o, pl.ds(0, slab), :],
-                dst_ref=outs[o].at[:, pl.ds(0, width)],
-                send_sem=send_sems.at[o, j], recv_sem=recv_sems.at[o, j],
-                device_id=(me_s, lax.rem(me + j, ne)), device_id_type=MESH,
-            )
-            cp.wait_send()
-            cp.wait_recv()
-        pltpu.make_async_copy(
-            stage.at[o, pl.ds(0, slab), :], outs[o].at[:, pl.ds(0, width)], local_sems.at[o]
-        ).wait()
+        for h in range(heads):
+            for j in range(1, ne):
+                cp = pltpu.make_async_remote_copy(
+                    src_ref=stage.at[o, pl.ds(0, slab), cols(h)],
+                    dst_ref=outs[o].at[:, pl.ds(h * hd, hd)],
+                    send_sem=send_sems.at[o, h, j], recv_sem=recv_sems.at[o, h, j],
+                    device_id=(me_s, lax.rem(me + j, ne)), device_id_type=MESH,
+                )
+                cp.wait_send()
+                cp.wait_recv()
+            pltpu.make_async_copy(
+                stage.at[o, pl.ds(0, slab), cols(h)], outs[o].at[:, pl.ds(h * hd, hd)], local_sems.at[o, h]
+            ).wait()
 
 
 def shards(query_tok, key_tok, value_tok, grad_out, decay_rate):
@@ -253,10 +248,10 @@
             pltpu.VMEM((4, seg_len, width), jnp.bfloat16),
             pltpu.VMEM((num_heads, seg_len, seg_len), jnp.bfloat16),
             pltpu.VMEM((num_heads, seg_len, seg_len), jnp.bfloat16),
-            pltpu.SemaphoreType.DMA((2, 2 * nrecv)),
-            pltpu.SemaphoreType.DMA((4, ne)),
-            pltpu.SemaphoreType.DMA((4, ne)),
-            pltpu.SemaphoreType.DMA((4,)),
+            pltpu.SemaphoreType.DMA((2, num_heads, 2 * nrecv)),
+            pltpu.SemaphoreType.DMA((4, num_heads, ne)),
+            pltpu.SemaphoreType.DMA((4, num_heads, ne)),
+            pltpu.SemaphoreType.DMA((4, num_heads)),
         ],
         compiler_params=pltpu.CompilerParams(
             collective_id=0, has_side_effects=True, vmem_limit_bytes=56 * 1024 * 1024

time: 118 us -> 107 us (0.907)
  the two profiles are of different devices: /device:TPU:83 before, /device:TPU:1 now
where the time goes in v5:
time: 107 us
  Pallas kernels  94.1 us (88%)
  local copies, waits for them, and re-layouts  8.93 us (8%)
  matrix products  1.91 us (2%)
  other arithmetic  1.42 us (1%)
    pallas_call x1, Pallas kernels, shards(): pl.pallas_call(functools.partial(whole_kernel, n, near, far), out_shape=(...  94.1 us
    unnamed x20, local copies, waits for them, and re-layouts  6.83 us

profile of v5, /device:TPU:1, one launch (start us, length us, event | category | flops | bytes accessed | tf_op | source)
XLA Modules:
  0.0 107.1 jit_solution(5686812996065350672)
XLA Ops:
  0.6 0.7 fusion.8
  1.3 0.7 copy-done.7
  2.0 0.6 pad_maximum_fusion.scal_ref
  2.5 0.1 copy-done.6
  2.6 0.1 multiply_exponential_fusion.2
  2.7 0.6 exp.22.w_ref
  3.3 0.1 multiply_exponential_fusion
  3.4 0.0 copy-start.2
  3.4 1.3 %copy.19 = f32[1024,256]{0,1:T(8,128)S(1)} copy(bf16[1024,256]{1,0:T(8,128)(2,1)} %q_ref.1) | data formatting | bytes 1572864 | tf_op jit(solution)/shard_map/convert_element_type | solution.py:209
  4.7 0.0 copy-done.2
  4.7 0.0 copy-start
  4.7 1.0 fusion.1.dq_ref
  5.7 0.1 copy-done
  5.8 0.2 copy.18
  6.0 0.8 copy-done.1
  6.8 1.0 fusion.dk_ref
  7.8 94.1 %shard_map.93 = (bf16[64,4096]{1,0:T(8,128)(2,1)}, bf16[64,4096]{1,0:T(8,128)(2,1)}, bf16[64,4096]{1,0:T(8,128)(2,1)}, bf16[64,4096]{1,0:T(8,128)(2,1)}) custom-call(f32[10]{0:T(128)} %exp.22.w_ref, f32[4]{0:T(128)} %pad_maximum_fusion.scal_ref, bf16[1024,256]{1,0:T(8,128)(2,1)} %q_ref.1, bf16[1024,256]{1,0:T(8,128)(2,1)} %k_ref.1, bf16[1024,256]{1,0:T(8,128)(2,1)} %v_ref.1, ...), custom_call_target="tpu_custom_call" | custom-call | tf_op jit(solution)/shard_map/pallas_call | solution.py:235
  101.9 0.0 copy-start.5
  101.9 1.9 %copy.34 = bf16[64,4096]{1,0:T(8,128)(2,1)} copy(bf16[64,4096]{1,0:T(8,128)(2,1)} %get-tuple-element.15) | data formatting | bytes 1048576
  103.8 0.8 copy.35
  104.6 0.4 copy-done.4
  105.0 0.8 copy.36
  105.8 0.4 copy-done.3
  106.3 0.8 copy.37
  (7 shorter events, 0.0 us)
Async XLA Ops:
  1.3 0.7 copy-start.7
  2.0 0.7 copy-start.6
  3.4 1.3 %copy-start.2 = (bf16[1024,256]{1,0:T(8,128)(2,1)S(1)}, bf16[1024,256]{1,0:T(8,128)(2,1)}, u32[]{:S(2)}) copy-start(bf16[1024,256]{1,0:T(8,128)(2,1)} %do_ref.1) | copy-start | bytes 1572868
  4.7 1.0 copy-start
  5.8 1.0 copy-start.1
  101.9 1.9 %copy-start.5 = (bf16[64,4096]{1,0:T(8,128)(2,1)S(1)}, bf16[64,4096]{1,0:T(8,128)(2,1)}, u32[]{:S(2)}) copy-start(bf16[64,4096]{1,0:T(8,128)(2,1)} %get-tuple-element.16) | copy-start | bytes 1572868
  103.8 1.2 %copy-start.4 = (bf16[64,4096]{1,0:T(8,128)(2,1)S(1)}, bf16[64,4096]{1,0:T(8,128)(2,1)}, u32[]{:S(2)}) copy-start(bf16[64,4096]{1,0:T(8,128)(2,1)} %get-tuple-element.17) | copy-start | bytes 1572868
  105.0 1.2 %copy-start.3 = (bf16[64,4096]{1,0:T(8,128)(2,1)S(1)}, bf16[64,4096]{1,0:T(8,128)(2,1)}, u32[]{:S(2)}) copy-start(bf16[64,4096]{1,0:T(8,128)(2,1)} %get-tuple-element.18) | copy-start | bytes 1572868

commit v6 on v5

--- a/solution.py
+++ b/solution.py
@@ -11,8 +11,8 @@
 MESH = pl.DeviceIdType.MESH
 
 
-def whole_kernel(n, near, far, w_ref, scal_ref, q_ref, k_ref, v_ref, do_ref, dk_ref, dq_ref,
-                 o0, o1, o2, o3, kx, qx, krecv, qrecv, s_acc, r_acc, intra, stage, wts, gwts,
+def whole_kernel(n, near, far, w_ref, scal_ref, q_ref, k_ref, v_ref, do_ref,
+                 o0, o1, o2, o3, dk_ref, dq_ref, kx, qx, krecv, qrecv, s_acc, r_acc, intra, stage, wts, gwts,
                  scan_sems, send_sems, recv_sems, local_sems):
     outs = (o0, o1, o2, o3)
     me_s = lax.axis_index("seq")
@@ -29,6 +29,17 @@
     nt = (((1,), (1,)), ((), ()))
     tn = (((0,), (0,)), ((), ()))
 
+    def cols(h):
+        return pl.ds(h * hd, hd)
+
+    place = lax.broadcasted_iota(jnp.int32, (length, 1), 0).astype(f32)
+    for h in range(heads):
+        rate = scal_ref[h]
+        keyed = (k_ref[:, cols(h)].astype(f32) * jnp.exp(-rate * (length - place))).astype(jnp.bfloat16)
+        dk_ref[h] = lax.dot_general(keyed, v_ref[:, cols(h)], tn, preferred_element_type=f32)
+        queried = (q_ref[:, cols(h)].astype(f32) * jnp.exp(-rate * (place + 1.0))).astype(jnp.bfloat16)
+        dq_ref[h] = lax.dot_general(queried, do_ref[:, cols(h)], tn, preferred_element_type=f32)
+
     barrier = pltpu.get_barrier_semaphore()
     partners = sorted(set(near + [1, far]))
     peers = ne - 1
@@ -41,9 +52,6 @@
     for j in range(1, ne):
         pl.semaphore_signal(barrier, 1, device_id=(me_s, lax.rem(me + j, ne)), device_id_type=MESH)
     pl.semaphore_wait(barrier, peers)
-
-    def cols(h):
-        return pl.ds(h * hd, hd)
 
     def weights_task(h):
         def run():
@@ -197,22 +205,6 @@
     ne = lax.axis_size("exp")
     total_len = seg_len * lax.axis_size("seq")
     scale_head = jnp.sqrt((2.0 * decay_rate + 2.0 / total_len) / head_size)
-    shape_three = (seg_len, num_heads, head_size)
-    query_heads = query_tok.reshape(shape_three)
-    key_heads = key_tok.reshape(shape_three)
-    value_heads = value_tok.reshape(shape_three)
-    upstream = grad_out.reshape(shape_three)
-    position = jnp.arange(seg_len, dtype=jnp.float32)
-    to_end = jnp.exp(-decay_rate[None, :] * (seg_len - position[:, None]))
-    from_start = jnp.exp(-decay_rate[None, :] * (position[:, None] + 1.0))
-    key_product = (key_heads * to_end[:, :, None]).astype(jnp.bfloat16)
-    query_product = (query_heads * from_start[:, :, None]).astype(jnp.bfloat16)
-    dev_key = jnp.einsum(
-        "ihd,ihe->hde", key_product, value_heads, preferred_element_type=jnp.float32
-    )
-    dev_query = jnp.einsum(
-        "ihd,ihe->hde", query_product, upstream, preferred_element_type=jnp.float32
-    )
     rate_len = decay_rate * seg_len
     n = lax.axis_size("seq")
     near = []
@@ -231,13 +223,15 @@
     smem = pl.BlockSpec(memory_space=pltpu.SMEM)
     vspec = pl.BlockSpec(memory_space=pltpu.VMEM)
     anyspec = pl.BlockSpec(memory_space=pl.ANY)
-    st = dev_key.shape
+    st = (num_heads, head_size, head_size)
     return pl.pallas_call(
         functools.partial(whole_kernel, n, near, far),
         out_shape=(out, out, out, out),
-        in_specs=[smem, smem] + [vspec] * 6,
+        in_specs=[smem, smem] + [vspec] * 4,
         out_specs=(anyspec, anyspec, anyspec, anyspec),
         scratch_shapes=[
+            pltpu.VMEM(st, jnp.float32),
+            pltpu.VMEM(st, jnp.float32),
             pltpu.VMEM((len(near),) + st, jnp.float32),
             pltpu.VMEM((len(near),) + st, jnp.float32),
             pltpu.VMEM((nrecv,) + st, jnp.float32),
@@ -256,7 +250,7 @@
         compiler_params=pltpu.CompilerParams(
             collective_id=0, has_side_effects=True, vmem_limit_bytes=56 * 1024 * 1024
         ),
-    )(weights, scalars, query_tok, key_tok, value_tok, grad_out, dev_key, dev_query)
+    )(weights, scalars, query_tok, key_tok, value_tok, grad_out)
 
 
 def solution(mesh):

time: 107 us -> 104 us (0.972)
  local copies, waits for them, and re-layouts: 8.93 us -> 6.51 us
  matrix products: 1.91 us -> 0 us
  Pallas kernels: 94.1 us -> 95.6 us
    dot_general x2 -> x0, matrix products: 1.91 us -> none  [the longest x1 0.96 us: shards(): jnp.einsum('ihd,ihe->hde', query_product, upstream, preferred_element_typ...]
    convert_element_type x2 -> x0, local copies, waits for them, and re-layouts: 1.51 us -> none  [the longest x1 1.3 us: shards(): query_product = (query_heads * from_start[:, :, None]).astype(jnp.bfloat16)]
    pallas_call x1, Pallas kernels: 94.1 us -> 95.6 us  [shards(): pl.pallas_call(functools.partial(whole_kernel, n, near, far), out_shape=(...]
    unnamed x20 -> x14, local copies, waits for them, and re-layouts: 6.83 us -> 5.91 us
where the time goes in v6:
time: 104 us
  Pallas kernels  95.6 us (92%)
  local copies, waits for them, and re-layouts  6.51 us (6%)
  other arithmetic  1.32 us (1%)
    pallas_call x1, Pallas kernels, shards(): pl.pallas_call(functools.partial(whole_kernel, n, near, far), out_shape=(...  95.6 us
    unnamed x14, local copies, waits for them, and re-layouts  5.91 us

profile of v6, /device:TPU:1, one launch (start us, length us, event | category | flops | bytes accessed | tf_op | source)
XLA Modules:
  0.0 104.1 jit_solution(639006412564447180)
XLA Ops:
  0.6 0.7 multiply_sqrt_fusion
  1.3 0.0 copy-start.4
  1.3 0.7 copy-done.4
  2.0 0.0 copy-start.3
  2.0 0.6 pad_maximum_fusion.scal_ref
  2.5 0.1 copy-done.3
  2.6 0.1 multiply_exponential_fusion
  2.7 0.6 exp.8.w_ref
  3.3 95.6 %shard_map.93 = (bf16[64,4096]{1,0:T(8,128)(2,1)}, bf16[64,4096]{1,0:T(8,128)(2,1)}, bf16[64,4096]{1,0:T(8,128)(2,1)}, bf16[64,4096]{1,0:T(8,128)(2,1)}) custom-call(f32[10]{0:T(128)} %exp.8.w_ref, f32[4]{0:T(128)} %pad_maximum_fusion.scal_ref, bf16[1024,256]{1,0:T(8,128)(2,1)} %q_ref.1, bf16[1024,256]{1,0:T(8,128)(2,1)} %k_ref.1, bf16[1024,256]{1,0:T(8,128)(2,1)} %v_ref.1, ...), custom_call_target="tpu_custom_call" | custom-call | tf_op jit(solution)/shard_map/pallas_call | solution.py:227
  98.9 0.0 copy-start.2
  98.9 1.9 %copy.14 = bf16[64,4096]{1,0:T(8,128)(2,1)} copy(bf16[64,4096]{1,0:T(8,128)(2,1)} %get-tuple-element.10) | data formatting | bytes 1048576
  100.8 0.0 copy-done.2
  100.8 0.0 copy-start.1
  100.8 0.8 copy.15
  101.6 0.4 copy-done.1
  102.0 0.0 copy-start
  102.0 0.8 copy.16
  102.8 0.4 copy-done
  103.3 0.8 copy.17
Async XLA Ops:
  1.3 0.7 copy-start.4
  2.0 0.7 copy-start.3
  98.9 1.9 %copy-start.2 = (bf16[64,4096]{1,0:T(8,128)(2,1)S(1)}, bf16[64,4096]{1,0:T(8,128)(2,1)}, u32[]{:S(2)}) copy-start(bf16[64,4096]{1,0:T(8,128)(2,1)} %get-tuple-element.11) | copy-start | bytes 1572868
  100.8 1.2 %copy-start.1 = (bf16[64,4096]{1,0:T(8,128)(2,1)S(1)}, bf16[64,4096]{1,0:T(8,128)(2,1)}, u32[]{:S(2)}) copy-start(bf16[64,4096]{1,0:T(8,128)(2,1)} %get-tuple-element.12) | copy-start | bytes 1572868
  102.0 1.2 %copy-start = (bf16[64,4096]{1,0:T(8,128)(2,1)S(1)}, bf16[64,4096]{1,0:T(8,128)(2,1)}, u32[]{:S(2)}) copy-start(bf16[64,4096]{1,0:T(8,128)(2,1)} %get-tuple-element.13) | copy-start | bytes 1572868

commit v7 on v6

--- a/solution.py
+++ b/solution.py
@@ -94,8 +94,14 @@
             device_id=(lax.rem(other + n, n), me), device_id_type=MESH,
         )
 
+    order = []
+    for j in range(1, ne):
+        for cand in (j, ne - j):
+            if 0 < cand < ne and cand not in order:
+                order.append(cand)
+
     def send(o, h):
-        for j in range(1, ne):
+        for j in order:
             peer = lax.rem(me + j, ne)
             pltpu.make_async_remote_copy(
                 src_ref=stage.at[o, pl.ds(pl.multiple_of(peer * slab, slab), slab), cols(h)],
@@ -115,6 +121,12 @@
     nround = len(near) + 1
     sent = []
     last = len(near)
+    pending = []
+
+    def flush_one():
+        if pending:
+            pending.pop(0)()
+
     for h in range(heads):
         mine = [weights_task(h)] + [intra_task(h, o) for o in range(4)]
         per_round = -(-len(mine) // nround)
@@ -126,6 +138,7 @@
             pl.when(me_s - d >= 0)(qc.start)
             sent.append((kc, me_s + d < n))
             sent.append((qc, me_s - d >= 0))
+            flush_one()
             for task in mine[r * per_round:(r + 1) * per_round]:
                 task()
             for cur, nxt, recv, cp, has in ((kcur, kx, krecv, kc, me_s - d >= 0), (qcur, qx, qrecv, qc, me_s + d < n)):
@@ -148,6 +161,7 @@
             sent.append((kc, me_s + d < n))
             sent.append((qc, me_s - d >= 0))
             finals.append((kc, qc, d))
+        flush_one()
         for task in mine[last * per_round:]:
             task()
         s_acc[h] = jnp.zeros((hd, hd), f32)
@@ -160,25 +174,37 @@
                     scale = 1.0 if j == 0 else w_ref[last * heads + h]
                     acc[h] = acc[h] + scale * recv[last + j, h]
 
-        rate = scal_ref[h]
-        scale = scal_ref[heads + h]
-        for o in range(4):
-            for b in range(nblk):
-                rows = pl.ds(b * blk, blk)
-                if o == 0:
-                    lead = scale * jnp.exp(-rate * pos(b))
-                    extra = lead * jnp.dot(q_ref[rows, cols(h)].astype(f32), s_acc[h], precision=hi, preferred_element_type=f32)
-                elif o == 1:
-                    lead = scale * jnp.exp(-rate * pos(b))
-                    extra = lead * lax.dot_general(do_ref[rows, cols(h)].astype(f32), s_acc[h], nt, precision=hi, preferred_element_type=f32)
-                elif o == 2:
-                    trail = scale * jnp.exp(-rate * (length - 1.0 - pos(b)))
-                    extra = trail * lax.dot_general(v_ref[rows, cols(h)].astype(f32), r_acc[h], nt, precision=hi, preferred_element_type=f32)
-                else:
-                    trail = scale * jnp.exp(-rate * (length - 1.0 - pos(b)))
-                    extra = trail * jnp.dot(k_ref[rows, cols(h)].astype(f32), r_acc[h], precision=hi, preferred_element_type=f32)
-                stage[o, rows, cols(h)] = (intra[o, rows, cols(h)] + extra).astype(jnp.bfloat16)
-            send(o, h)
+        def stage_send(h, o):
+            def run():
+                rate = scal_ref[h]
+                scale = scal_ref[heads + h]
+                for b in range(nblk):
+                    rows = pl.ds(b * blk, blk)
+                    if o == 0:
+                        lead = scale * jnp.exp(-rate * pos(b))
+                        extra = lead * jnp.dot(q_ref[rows, cols(h)].astype(f32), s_acc[h], precision=hi, preferred_element_type=f32)
+                    elif o == 1:
+                        lead = scale * jnp.exp(-rate * pos(b))
+                        extra = lead * lax.dot_general(do_ref[rows, cols(h)].astype(f32), s_acc[h], nt, precision=hi, preferred_element_type=f32)
+                    elif o == 2:
+                        trail = scale * jnp.exp(-rate * (length - 1.0 - pos(b)))
+                        extra = trail * lax.dot_general(v_ref[rows, cols(h)].astype(f32), r_acc[h], nt, precision=hi, preferred_element_type=f32)
+                    else:
+                        trail = scale * jnp.exp(-rate * (length - 1.0 - pos(b)))
+                        extra = trail * jnp.dot(k_ref[rows, cols(h)].astype(f32), r_acc[h], precision=hi, preferred_element_type=f32)
+                    stage[o, rows, cols(h)] = (intra[o, rows, cols(h)] + extra).astype(jnp.bfloat16)
+                send(o, h)
+            return run
+
+        batches = [stage_send(h, o) for o in range(4)]
+        if h < heads - 1:
+            batches[0]()
+            pending.extend(batches[1:])
+        else:
+            while pending:
+                flush_one()
+            for run in batches:
+                run()
 
     for cp, cond in sent:
         pl.when(cond)(cp.wait_send)

time: 104 us -> 102 us (0.981)
  Pallas kernels: 95.6 us -> 92.8 us
    pallas_call x1, Pallas kernels: 95.6 us -> 92.8 us  [shards(): pl.pallas_call(functools.partial(whole_kernel, n, near, far), out_shape=(...]
where the time goes in v7:
time: 102 us; the launch traced here: 101 us
  Pallas kernels  92.8 us (91%)
  local copies, waits for them, and re-layouts  6.51 us (6%)
  other arithmetic  1.32 us (1%)
    pallas_call x1, Pallas kernels, shards(): pl.pallas_call(functools.partial(whole_kernel, n, near, far), out_shape=(...  92.8 us
    unnamed x14, local copies, waits for them, and re-layouts  5.91 us

profile of v7, /device:TPU:1, one launch (start us, length us, event | category | flops | bytes accessed | tf_op | source)
XLA Modules:
  0.0 101.3 jit_solution(9766980505817009225)
XLA Ops:
  0.6 0.7 multiply_sqrt_fusion
  1.3 0.0 copy-start.4
  1.3 0.7 copy-done.4
  2.0 0.0 copy-start.3
  2.0 0.6 pad_maximum_fusion.scal_ref
  2.5 0.1 copy-done.3
  2.6 0.1 multiply_exponential_fusion
  2.7 0.6 exp.8.w_ref
  3.3 92.8 %shard_map.93 = (bf16[64,4096]{1,0:T(8,128)(2,1)}, bf16[64,4096]{1,0:T(8,128)(2,1)}, bf16[64,4096]{1,0:T(8,128)(2,1)}, bf16[64,4096]{1,0:T(8,128)(2,1)}) custom-call(f32[10]{0:T(128)} %exp.8.w_ref, f32[4]{0:T(128)} %pad_maximum_fusion.scal_ref, bf16[1024,256]{1,0:T(8,128)(2,1)} %q_ref.1, bf16[1024,256]{1,0:T(8,128)(2,1)} %k_ref.1, bf16[1024,256]{1,0:T(8,128)(2,1)} %v_ref.1, ...), custom_call_target="tpu_custom_call" | custom-call | tf_op jit(solution)/shard_map/pallas_call | solution.py:253
  96.1 0.0 copy-start.2
  96.1 1.9 %copy.14 = bf16[64,4096]{1,0:T(8,128)(2,1)} copy(bf16[64,4096]{1,0:T(8,128)(2,1)} %get-tuple-element.10) | data formatting | bytes 1048576
  98.1 0.0 copy-done.2
  98.1 0.0 copy-start.1
  98.1 0.8 copy.15
  98.9 0.4 copy-done.1
  99.3 0.0 copy-start
  99.3 0.8 copy.16
  100.1 0.4 copy-done
  100.5 0.8 copy.17
Async XLA Ops:
  1.3 0.7 copy-start.4
  2.0 0.7 copy-start.3
  96.1 1.9 %copy-start.2 = (bf16[64,4096]{1,0:T(8,128)(2,1)S(1)}, bf16[64,4096]{1,0:T(8,128)(2,1)}, u32[]{:S(2)}) copy-start(bf16[64,4096]{1,0:T(8,128)(2,1)} %get-tuple-element.11) | copy-start | bytes 1572868
  98.1 1.2 %copy-start.1 = (bf16[64,4096]{1,0:T(8,128)(2,1)S(1)}, bf16[64,4096]{1,0:T(8,128)(2,1)}, u32[]{:S(2)}) copy-start(bf16[64,4096]{1,0:T(8,128)(2,1)} %get-tuple-element.12) | copy-start | bytes 1572868
  99.3 1.2 %copy-start = (bf16[64,4096]{1,0:T(8,128)(2,1)S(1)}, bf16[64,4096]{1,0:T(8,128)(2,1)}, u32[]{:S(2)}) copy-start(bf16[64,4096]{1,0:T(8,128)(2,1)} %get-tuple-element.13) | copy-start | bytes 1572868

commit v8 on v7

--- a/solution.py
+++ b/solution.py
@@ -11,15 +11,18 @@
 MESH = pl.DeviceIdType.MESH
 
 
-def whole_kernel(n, near, far, w_ref, scal_ref, q_ref, k_ref, v_ref, do_ref,
+def whole_kernel(n, near, far, packed, q_ref, k_ref, v_ref, do_ref,
                  o0, o1, o2, o3, dk_ref, dq_ref, kx, qx, krecv, qrecv, s_acc, r_acc, intra, stage, wts, gwts,
                  scan_sems, send_sems, recv_sems, local_sems):
     outs = (o0, o1, o2, o3)
+    heads = dk_ref.shape[0]
+    nw = (len(near) + 1) * heads
+    w_ref = packed
+    scal_ref = packed.at[pl.ds(nw, 2 * heads)]
     me_s = lax.axis_index("seq")
     me = lax.axis_index("exp")
     ne = lax.axis_size("exp")
     length, width = q_ref.shape
-    heads = scal_ref.shape[0] // 2
     hd = width // heads
     slab = length // ne
     blk = min(256, length)
@@ -242,7 +245,7 @@
     dists = jnp.asarray(near + [d], jnp.float32)
     weights = jnp.exp(-dists[:, None] * rate_len[None, :]).reshape(-1)
     nrecv = len(near) + 2
-    scalars = jnp.concatenate([decay_rate, scale_head]).astype(jnp.float32)
+    packed = jnp.concatenate([weights, decay_rate, scale_head]).astype(jnp.float32)
     width = query_tok.shape[1]
     slab = seg_len // ne
     out = jax.ShapeDtypeStruct((slab, ne * width), jnp.bfloat16)
@@ -253,7 +256,7 @@
     return pl.pallas_call(
         functools.partial(whole_kernel, n, near, far),
         out_shape=(out, out, out, out),
-        in_specs=[smem, smem] + [vspec] * 4,
+        in_specs=[smem] + [vspec] * 4,
         out_specs=(anyspec, anyspec, anyspec, anyspec),
         scratch_shapes=[
             pltpu.VMEM(st, jnp.float32),
@@ -276,7 +279,7 @@
         compiler_params=pltpu.CompilerParams(
             collective_id=0, has_side_effects=True, vmem_limit_bytes=56 * 1024 * 1024
         ),
-    )(weights, scalars, query_tok, key_tok, value_tok, grad_out)
+    )(packed, query_tok, key_tok, value_tok, grad_out)
 
 
 def solution(mesh):

time: 102 us -> 102 us (level)
  no operation moved by 1% of the time
where the time goes in v8:
time: 102 us; the launch traced here: 101 us
  Pallas kernels  92.9 us (91%)
  local copies, waits for them, and re-layouts  6.5 us (6%)
  other arithmetic  1.32 us (1%)
    pallas_call x1, Pallas kernels, shards(): pl.pallas_call(functools.partial(whole_kernel, n, near, far), out_shape=(...  92.9 us
    unnamed x14, local copies, waits for them, and re-layouts  6.42 us

profile of v8, /device:TPU:1, one launch (start us, length us, event | category | flops | bytes accessed | tf_op | source)
XLA Modules:
  0.0 101.3 jit_solution(16003612631479562229)
XLA Ops:
  0.6 0.7 broadcast_multiply_fusion
  1.3 0.0 copy-start.3
  1.3 0.7 copy-done.3
  2.0 0.1 multiply_exponential_fusion
  2.0 0.0 copy-start.4
  2.0 0.1 exp.8
  2.1 0.6 copy-done.4
  2.7 0.6 pad_maximum_fusion.packed
  3.3 92.9 %shard_map.93 = (bf16[64,4096]{1,0:T(8,128)(2,1)}, bf16[64,4096]{1,0:T(8,128)(2,1)}, bf16[64,4096]{1,0:T(8,128)(2,1)}, bf16[64,4096]{1,0:T(8,128)(2,1)}) custom-call(f32[14]{0:T(128)} %pad_maximum_fusion.packed, bf16[1024,256]{1,0:T(8,128)(2,1)} %q_ref.1, bf16[1024,256]{1,0:T(8,128)(2,1)} %k_ref.1, bf16[1024,256]{1,0:T(8,128)(2,1)} %v_ref.1, ...), custom_call_target="tpu_custom_call" | custom-call | tf_op jit(solution)/shard_map/pallas_call | solution.py:256
  96.1 0.0 copy-start.2
  96.1 1.9 %copy.14 = bf16[64,4096]{1,0:T(8,128)(2,1)} copy(bf16[64,4096]{1,0:T(8,128)(2,1)} %get-tuple-element.10) | data formatting | bytes 1048576
  98.1 0.0 copy-done.2
  98.1 0.0 copy-start.1
  98.1 0.8 copy.15
  98.9 0.4 copy-done.1
  99.3 0.0 copy-start
  99.3 0.8 copy.16
  100.1 0.4 copy-done
  100.5 0.8 copy.17
Async XLA Ops:
  1.3 0.7 copy-start.3
  2.0 0.7 copy-start.4
  96.1 1.9 %copy-start.2 = (bf16[64,4096]{1,0:T(8,128)(2,1)S(1)}, bf16[64,4096]{1,0:T(8,128)(2,1)}, u32[]{:S(2)}) copy-start(bf16[64,4096]{1,0:T(8,128)(2,1)} %get-tuple-element.11) | copy-start | bytes 1572868
  98.1 1.2 %copy-start.1 = (bf16[64,4096]{1,0:T(8,128)(2,1)S(1)}, bf16[64,4096]{1,0:T(8,128)(2,1)}, u32[]{:S(2)}) copy-start(bf16[64,4096]{1,0:T(8,128)(2,1)} %get-tuple-element.12) | copy-start | bytes 1572868
  99.3 1.2 %copy-start = (bf16[64,4096]{1,0:T(8,128)(2,1)S(1)}, bf16[64,4096]{1,0:T(8,128)(2,1)}, u32[]{:S(2)}) copy-start(bf16[64,4096]{1,0:T(8,128)(2,1)} %get-tuple-element.13) | copy-start | bytes 1572868

commit v9 on v8

--- a/solution.py
+++ b/solution.py
@@ -130,17 +130,32 @@
         if pending:
             pending.pop(0)()
 
+    early = {}
+
+    def first_round(h):
+        d = near[0]
+        kc = copy(dk_ref.at[h], krecv.at[0, h], h, 0, me_s + d)
+        qc = copy(dq_ref.at[h], qrecv.at[0, h], h, 1, me_s - d)
+        pl.when(me_s + d < n)(kc.start)
+        pl.when(me_s - d >= 0)(qc.start)
+        sent.append((kc, me_s + d < n))
+        sent.append((qc, me_s - d >= 0))
+        return kc, qc
+
     for h in range(heads):
         mine = [weights_task(h)] + [intra_task(h, o) for o in range(4)]
         per_round = -(-len(mine) // nround)
         kcur, qcur = dk_ref.at[h], dq_ref.at[h]
         for r, d in enumerate(near):
-            kc = copy(kcur, krecv.at[r, h], h, 2 * r, me_s + d)
-            qc = copy(qcur, qrecv.at[r, h], h, 2 * r + 1, me_s - d)
-            pl.when(me_s + d < n)(kc.start)
-            pl.when(me_s - d >= 0)(qc.start)
-            sent.append((kc, me_s + d < n))
-            sent.append((qc, me_s - d >= 0))
+            if r == 0:
+                kc, qc = early.pop(h) if h in early else first_round(h)
+            else:
+                kc = copy(kcur, krecv.at[r, h], h, 2 * r, me_s + d)
+                qc = copy(qcur, qrecv.at[r, h], h, 2 * r + 1, me_s - d)
+                pl.when(me_s + d < n)(kc.start)
+                pl.when(me_s - d >= 0)(qc.start)
+                sent.append((kc, me_s + d < n))
+                sent.append((qc, me_s - d >= 0))
             flush_one()
             for task in mine[r * per_round:(r + 1) * per_round]:
                 task()
@@ -164,6 +179,8 @@
             sent.append((kc, me_s + d < n))
             sent.append((qc, me_s - d >= 0))
             finals.append((kc, qc, d))
+        if near and h + 1 < heads:
+            early[h + 1] = first_round(h + 1)
         flush_one()
         for task in mine[last * per_round:]:
             task()

time: 102 us -> 101 us (level)
  no operation moved by 1% of the time
where the time goes in v9:
time: 101 us
  Pallas kernels  92.6 us (92%)
  local copies, waits for them, and re-layouts  6.5 us (6%)
  other arithmetic  1.32 us (1%)
    pallas_call x1, Pallas kernels, shards(): pl.pallas_call(functools.partial(whole_kernel, n, near, far), out_shape=(...  92.6 us
    unnamed x14, local copies, waits for them, and re-layouts  6.42 us

profile of v9, /device:TPU:1, one launch (start us, length us, event | category | flops | bytes accessed | tf_op | source)
XLA Modules:
  0.0 101.1 jit_solution(10617190652511797288)
XLA Ops:
  0.6 0.7 broadcast_multiply_fusion
  1.3 0.0 copy-start.3
  1.3 0.7 copy-done.3
  2.0 0.1 multiply_exponential_fusion
  2.0 0.0 copy-start.4
  2.0 0.1 exp.8
  2.1 0.6 copy-done.4
  2.7 0.6 pad_maximum_fusion.packed
  3.3 92.6 %shard_map.93 = (bf16[64,4096]{1,0:T(8,128)(2,1)}, bf16[64,4096]{1,0:T(8,128)(2,1)}, bf16[64,4096]{1,0:T(8,128)(2,1)}, bf16[64,4096]{1,0:T(8,128)(2,1)}) custom-call(f32[14]{0:T(128)} %pad_maximum_fusion.packed, bf16[1024,256]{1,0:T(8,128)(2,1)} %q_ref.1, bf16[1024,256]{1,0:T(8,128)(2,1)} %k_ref.1, bf16[1024,256]{1,0:T(8,128)(2,1)} %v_ref.1, ...), custom_call_target="tpu_custom_call" | custom-call | tf_op jit(solution)/shard_map/pallas_call | solution.py:273
  95.9 0.0 copy-start.2
  95.9 1.9 %copy.14 = bf16[64,4096]{1,0:T(8,128)(2,1)} copy(bf16[64,4096]{1,0:T(8,128)(2,1)} %get-tuple-element.10) | data formatting | bytes 1048576
  97.9 0.0 copy-done.2
  97.9 0.0 copy-start.1
  97.9 0.8 copy.15
  98.6 0.4 copy-done.1
  99.1 0.0 copy-start
  99.1 0.8 copy.16
  99.9 0.4 copy-done
  100.3 0.8 copy.17
Async XLA Ops:
  1.3 0.7 copy-start.3
  2.0 0.7 copy-start.4
  95.9 1.9 %copy-start.2 = (bf16[64,4096]{1,0:T(8,128)(2,1)S(1)}, bf16[64,4096]{1,0:T(8,128)(2,1)}, u32[]{:S(2)}) copy-start(bf16[64,4096]{1,0:T(8,128)(2,1)} %get-tuple-element.11) | copy-start | bytes 1572868
  97.9 1.2 %copy-start.1 = (bf16[64,4096]{1,0:T(8,128)(2,1)S(1)}, bf16[64,4096]{1,0:T(8,128)(2,1)}, u32[]{:S(2)}) copy-start(bf16[64,4096]{1,0:T(8,128)(2,1)} %get-tuple-element.12) | copy-start | bytes 1572868
  99.1 1.2 %copy-start = (bf16[64,4096]{1,0:T(8,128)(2,1)S(1)}, bf16[64,4096]{1,0:T(8,128)(2,1)}, u32[]{:S(2)}) copy-start(bf16[64,4096]{1,0:T(8,128)(2,1)} %get-tuple-element.13) | copy-start | bytes 1572868

commit v10 on v9

--- a/solution.py
+++ b/solution.py
@@ -143,7 +143,8 @@
         return kc, qc
 
     for h in range(heads):
-        mine = [weights_task(h)] + [intra_task(h, o) for o in range(4)]
+        later = 2 if h < heads - 1 else 4
+        mine = [weights_task(h)] + [intra_task(h, o) for o in range(later)]
         per_round = -(-len(mine) // nround)
         kcur, qcur = dk_ref.at[h], dq_ref.at[h]
         for r, d in enumerate(near):
@@ -216,7 +217,13 @@
                 send(o, h)
             return run
 
-        batches = [stage_send(h, o) for o in range(4)]
+        def both(first, second):
+            def run():
+                first()
+                second()
+            return run
+
+        batches = [stage_send(h, o) if o < later else both(intra_task(h, o), stage_send(h, o)) for o in range(4)]
         if h < heads - 1:
             batches[0]()
             pending.extend(batches[1:])

time: 101 us -> 102 us (level); the launches traced: 101 us -> 101 us
  no operation moved by 1% of the time
where the time goes in v10:
time: 102 us; the launch traced here: 101 us
  Pallas kernels  92.3 us (90%)
  local copies, waits for them, and re-layouts  6.5 us (6%)
  other arithmetic  1.32 us (1%)
    pallas_call x1, Pallas kernels, shards(): pl.pallas_call(functools.partial(whole_kernel, n, near, far), out_shape=(...  92.3 us
    unnamed x14, local copies, waits for them, and re-layouts  6.42 us

profile of v10, /device:TPU:1, one launch (start us, length us, event | category | flops | bytes accessed | tf_op | source)
XLA Modules:
  0.0 100.8 jit_solution(16494097763244913849)
XLA Ops:
  0.6 0.7 broadcast_multiply_fusion
  1.3 0.0 copy-start.3
  1.3 0.7 copy-done.3
  2.0 0.1 multiply_exponential_fusion
  2.0 0.0 copy-start.4
  2.0 0.1 exp.8
  2.1 0.6 copy-done.4
  2.7 0.6 pad_maximum_fusion.packed
  3.3 92.3 %shard_map.93 = (bf16[64,4096]{1,0:T(8,128)(2,1)}, bf16[64,4096]{1,0:T(8,128)(2,1)}, bf16[64,4096]{1,0:T(8,128)(2,1)}, bf16[64,4096]{1,0:T(8,128)(2,1)}) custom-call(f32[14]{0:T(128)} %pad_maximum_fusion.packed, bf16[1024,256]{1,0:T(8,128)(2,1)} %q_ref.1, bf16[1024,256]{1,0:T(8,128)(2,1)} %k_ref.1, bf16[1024,256]{1,0:T(8,128)(2,1)} %v_ref.1, ...), custom_call_target="tpu_custom_call" | custom-call | tf_op jit(solution)/shard_map/pallas_call | solution.py:280
  95.6 0.0 copy-start.2
  95.6 1.9 %copy.14 = bf16[64,4096]{1,0:T(8,128)(2,1)} copy(bf16[64,4096]{1,0:T(8,128)(2,1)} %get-tuple-element.10) | data formatting | bytes 1048576
  97.6 0.0 copy-done.2
  97.6 0.0 copy-start.1
  97.6 0.8 copy.15
  98.4 0.4 copy-done.1
  98.8 0.0 copy-start
  98.8 0.8 copy.16
  99.6 0.4 copy-done
  100.0 0.8 copy.17
Async XLA Ops:
  1.3 0.7 copy-start.3
  2.0 0.7 copy-start.4
  95.6 1.9 %copy-start.2 = (bf16[64,4096]{1,0:T(8,128)(2,1)S(1)}, bf16[64,4096]{1,0:T(8,128)(2,1)}, u32[]{:S(2)}) copy-start(bf16[64,4096]{1,0:T(8,128)(2,1)} %get-tuple-element.11) | copy-start | bytes 1572868
  97.6 1.2 %copy-start.1 = (bf16[64,4096]{1,0:T(8,128)(2,1)S(1)}, bf16[64,4096]{1,0:T(8,128)(2,1)}, u32[]{:S(2)}) copy-start(bf16[64,4096]{1,0:T(8,128)(2,1)} %get-tuple-element.12) | copy-start | bytes 1572868
  98.8 1.2 %copy-start = (bf16[64,4096]{1,0:T(8,128)(2,1)S(1)}, bf16[64,4096]{1,0:T(8,128)(2,1)}, u32[]{:S(2)}) copy-start(bf16[64,4096]{1,0:T(8,128)(2,1)} %get-tuple-element.13) | copy-start | bytes 1572868

commit v11 on v7

--- a/solution.py
+++ b/solution.py
@@ -11,7 +11,7 @@
 MESH = pl.DeviceIdType.MESH
 
 
-def whole_kernel(n, near, far, w_ref, scal_ref, q_ref, k_ref, v_ref, do_ref,
+def whole_kernel(n, near, far, top, total, dec_ref, q_ref, k_ref, v_ref, do_ref,
                  o0, o1, o2, o3, dk_ref, dq_ref, kx, qx, krecv, qrecv, s_acc, r_acc, intra, stage, wts, gwts,
                  scan_sems, send_sems, recv_sems, local_sems):
     outs = (o0, o1, o2, o3)
@@ -19,7 +19,7 @@
     me = lax.axis_index("exp")
     ne = lax.axis_size("exp")
     length, width = q_ref.shape
-    heads = scal_ref.shape[0] // 2
+    heads = dec_ref.shape[0]
     hd = width // heads
     slab = length // ne
     blk = min(256, length)
@@ -32,9 +32,12 @@
     def cols(h):
         return pl.ds(h * hd, hd)
 
+    rates = [jnp.full((1, 1), dec_ref[h], f32) for h in range(heads)]
+    scales = [jnp.sqrt((2.0 * rates[h] + 2.0 / total) / hd) for h in range(heads)]
+    wv = [[jnp.exp(-float(d) * (rates[h] * float(length))) for h in range(heads)] for d in near + [top]]
     place = lax.broadcasted_iota(jnp.int32, (length, 1), 0).astype(f32)
     for h in range(heads):
-        rate = scal_ref[h]
+        rate = rates[h]
         keyed = (k_ref[:, cols(h)].astype(f32) * jnp.exp(-rate * (length - place))).astype(jnp.bfloat16)
         dk_ref[h] = lax.dot_general(keyed, v_ref[:, cols(h)], tn, preferred_element_type=f32)
         queried = (q_ref[:, cols(h)].astype(f32) * jnp.exp(-rate * (place + 1.0))).astype(jnp.bfloat16)
@@ -55,8 +58,8 @@
 
     def weights_task(h):
         def run():
-            rate = scal_ref[h]
-            scale = scal_ref[heads + h]
+            rate = rates[h]
+            scale = scales[h]
             qh = q_ref[:, cols(h)]
             kh = k_ref[:, cols(h)]
             vh = v_ref[:, cols(h)]
@@ -145,7 +148,7 @@
                 @pl.when(has)
                 def _():
                     cp.wait_recv()
-                    nxt[r, h] = cur[...] + w_ref[r * heads + h] * recv[r, h]
+                    nxt[r, h] = cur[...] + wv[r][h] * recv[r, h]
 
                 @pl.when(jnp.logical_not(has))
                 def _():
@@ -171,13 +174,13 @@
                 @pl.when(has)
                 def _():
                     cp.wait_recv()
-                    scale = 1.0 if j == 0 else w_ref[last * heads + h]
+                    scale = 1.0 if j == 0 else wv[last][h]
                     acc[h] = acc[h] + scale * recv[last + j, h]
 
         def stage_send(h, o):
             def run():
-                rate = scal_ref[h]
-                scale = scal_ref[heads + h]
+                rate = rates[h]
+                scale = scales[h]
                 for b in range(nblk):
                     rows = pl.ds(b * blk, blk)
                     if o == 0:
@@ -230,8 +233,6 @@
     head_size = query_tok.shape[1] // num_heads
     ne = lax.axis_size("exp")
     total_len = seg_len * lax.axis_size("seq")
-    scale_head = jnp.sqrt((2.0 * decay_rate + 2.0 / total_len) / head_size)
-    rate_len = decay_rate * seg_len
     n = lax.axis_size("seq")
     near = []
     d = 1
@@ -239,10 +240,7 @@
         near.append(d)
         d *= 2
     far = d + 1
-    dists = jnp.asarray(near + [d], jnp.float32)
-    weights = jnp.exp(-dists[:, None] * rate_len[None, :]).reshape(-1)
     nrecv = len(near) + 2
-    scalars = jnp.concatenate([decay_rate, scale_head]).astype(jnp.float32)
     width = query_tok.shape[1]
     slab = seg_len // ne
     out = jax.ShapeDtypeStruct((slab, ne * width), jnp.bfloat16)
@@ -251,9 +249,9 @@
     anyspec = pl.BlockSpec(memory_space=pl.ANY)
     st = (num_heads, head_size, head_size)
     return pl.pallas_call(
-        functools.partial(whole_kernel, n, near, far),
+        functools.partial(whole_kernel, n, near, far, d, total_len),
         out_shape=(out, out, out, out),
-        in_specs=[smem, smem] + [vspec] * 4,
+        in_specs=[smem] + [vspec] * 4,
         out_specs=(anyspec, anyspec, anyspec, anyspec),
         scratch_shapes=[
             pltpu.VMEM(st, jnp.float32),
@@ -276,7 +274,7 @@
         compiler_params=pltpu.CompilerParams(
             collective_id=0, has_side_effects=True, vmem_limit_bytes=56 * 1024 * 1024
         ),
-    )(weights, scalars, query_tok, key_tok, value_tok, grad_out)
+    )(decay_rate.astype(jnp.float32), query_tok, key_tok, value_tok, grad_out)
 
 
 def solution(mesh):

time: 102 us -> 99.6 us (0.976)
  local copies, waits for them, and re-layouts: 6.51 us -> 5.18 us
  other arithmetic: 1.32 us -> 0 us
    unnamed x14 -> x10, local copies, waits for them, and re-layouts: 5.91 us -> 5.18 us
where the time goes in v11:
time: 99.6 us; the launch traced here: 99.3 us
  Pallas kernels  93.5 us (94%)
  local copies, waits for them, and re-layouts  5.18 us (5%)
    pallas_call x1, Pallas kernels, shards(): pl.pallas_call(functools.partial(whole_kernel, n, near, far, d, total_len...  93.5 us
    unnamed x10, local copies, waits for them, and re-layouts  5.18 us

profile of v11, /device:TPU:1, one launch (start us, length us, event | category | flops | bytes accessed | tf_op | source)
XLA Modules:
  0.0 99.3 jit_solution(1984974962924916079)
XLA Ops:
  0.6 93.5 %shard_map.84 = (bf16[64,4096]{1,0:T(8,128)(2,1)}, bf16[64,4096]{1,0:T(8,128)(2,1)}, bf16[64,4096]{1,0:T(8,128)(2,1)}, bf16[64,4096]{1,0:T(8,128)(2,1)}) custom-call(f32[2]{0:T(128)} %dec_ref.1, bf16[1024,256]{1,0:T(8,128)(2,1)} %q_ref.1, bf16[1024,256]{1,0:T(8,128)(2,1)} %k_ref.1, bf16[1024,256]{1,0:T(8,128)(2,1)} %v_ref.1, bf16[1024,256]{1,0:T(8,128)(2,1)} %do_ref.1), custom_call_target="tpu_custom_call" | custom-call | tf_op jit(solution)/shard_map/pallas_call | solution.py:251
  94.2 0.0 copy-start.2
  94.2 1.9 %copy.13 = bf16[64,4096]{1,0:T(8,128)(2,1)} copy(bf16[64,4096]{1,0:T(8,128)(2,1)} %get-tuple-element.8) | data formatting | bytes 1048576
  96.1 0.0 copy-done.2
  96.1 0.0 copy-start.1
  96.1 0.8 copy.14
  96.9 0.4 copy-done.1
  97.3 0.0 copy-start
  97.3 0.8 copy.15
  98.1 0.4 copy-done
  98.6 0.8 copy.16
Async XLA Ops:
  94.2 1.9 %copy-start.2 = (bf16[64,4096]{1,0:T(8,128)(2,1)S(1)}, bf16[64,4096]{1,0:T(8,128)(2,1)}, u32[]{:S(2)}) copy-start(bf16[64,4096]{1,0:T(8,128)(2,1)} %get-tuple-element.9) | copy-start | bytes 1572868
  96.1 1.2 %copy-start.1 = (bf16[64,4096]{1,0:T(8,128)(2,1)S(1)}, bf16[64,4096]{1,0:T(8,128)(2,1)}, u32[]{:S(2)}) copy-start(bf16[64,4096]{1,0:T(8,128)(2,1)} %get-tuple-element.10) | copy-start | bytes 1572868
  97.3 1.2 %copy-start = (bf16[64,4096]{1,0:T(8,128)(2,1)S(1)}, bf16[64,4096]{1,0:T(8,128)(2,1)}, u32[]{:S(2)}) copy-start(bf16[64,4096]{1,0:T(8,128)(2,1)} %get-tuple-element.11) | copy-start | bytes 1572868

commit v12 on v11

--- a/solution.py
+++ b/solution.py
@@ -227,6 +227,11 @@
             ).wait()
 
 
+def settle_kernel(a, b, c, d, oa, ob, oc, od):
+    for src, dst in ((a, oa), (b, ob), (c, oc), (d, od)):
+        dst[...] = src[...]
+
+
 def shards(query_tok, key_tok, value_tok, grad_out, decay_rate):
     seg_len = query_tok.shape[0]
     num_heads = decay_rate.shape[0]
@@ -248,7 +253,7 @@
     vspec = pl.BlockSpec(memory_space=pltpu.VMEM)
     anyspec = pl.BlockSpec(memory_space=pl.ANY)
     st = (num_heads, head_size, head_size)
-    return pl.pallas_call(
+    moved = pl.pallas_call(
         functools.partial(whole_kernel, n, near, far, d, total_len),
         out_shape=(out, out, out, out),
         in_specs=[smem] + [vspec] * 4,
@@ -275,6 +280,12 @@
             collective_id=0, has_side_effects=True, vmem_limit_bytes=56 * 1024 * 1024
         ),
     )(decay_rate.astype(jnp.float32), query_tok, key_tok, value_tok, grad_out)
+    return pl.pallas_call(
+        settle_kernel,
+        out_shape=(out, out, out, out),
+        in_specs=[vspec] * 4,
+        out_specs=(vspec, vspec, vspec, vspec),
+    )(*moved)
 
 
 def solution(mesh):

time: 99.6 us -> 97.2 us (0.976)
  local copies, waits for them, and re-layouts: 5.18 us -> 0 us
  Pallas kernels: 93.5 us -> 96.4 us
    unnamed x10 -> x0, local copies, waits for them, and re-layouts: 5.18 us -> none
    pallas_call x0 -> x1, Pallas kernels: none -> 2.86 us  [shards(): pl.pallas_call(settle_kernel, out_shape=(out, out, out, out), in_specs=[v...]
where the time goes in v12:
time: 97.2 us; the launch traced here: 97 us
  Pallas kernels  96.4 us (99%)
    pallas_call x1, Pallas kernels, shards(): pl.pallas_call(functools.partial(whole_kernel, n, near, far, d, total_len...  93.5 us
    pallas_call x1, Pallas kernels, shards(): pl.pallas_call(settle_kernel, out_shape=(out, out, out, out), in_specs=[v...  2.86 us

profile of v12, /device:TPU:1, one launch (start us, length us, event | category | flops | bytes accessed | tf_op | source)
XLA Modules:
  0.0 97.0 jit_solution(18249372435446111845)
XLA Ops:
  0.6 93.5 %shard_map.84 = (bf16[64,4096]{1,0:T(8,128)(2,1)}, bf16[64,4096]{1,0:T(8,128)(2,1)}, bf16[64,4096]{1,0:T(8,128)(2,1)}, bf16[64,4096]{1,0:T(8,128)(2,1)}) custom-call(f32[2]{0:T(128)} %dec_ref.1, bf16[1024,256]{1,0:T(8,128)(2,1)} %q_ref.1, bf16[1024,256]{1,0:T(8,128)(2,1)} %k_ref.1, bf16[1024,256]{1,0:T(8,128)(2,1)} %v_ref.1, bf16[1024,256]{1,0:T(8,128)(2,1)} %do_ref.1), custom_call_target="tpu_custom_call" | custom-call | tf_op jit(solution)/shard_map/pallas_call | solution.py:256
  94.2 2.9 %shard_map.85 = (bf16[64,4096]{1,0:T(8,128)(2,1)}, bf16[64,4096]{1,0:T(8,128)(2,1)}, bf16[64,4096]{1,0:T(8,128)(2,1)}, bf16[64,4096]{1,0:T(8,128)(2,1)}) custom-call(bf16[64,4096]{1,0:T(8,128)(2,1)} %get-tuple-element.8.a, bf16[64,4096]{1,0:T(8,128)(2,1)} %get-tuple-element.9.b, bf16[64,4096]{1,0:T(8,128)(2,1)} %get-tuple-element.10.c, ...), custom_call_target="tpu_custom_call" | custom-call | tf_op jit(solution)/shard_map/pallas_call | solution.py:283

commit v13 on v12

--- a/solution.py
+++ b/solution.py
@@ -227,9 +227,19 @@
             ).wait()
 
 
-def settle_kernel(a, b, c, d, oa, ob, oc, od):
-    for src, dst in ((a, oa), (b, ob), (c, oc), (d, od)):
-        dst[...] = src[...]
+def settle_kernel(a, b, c, d, oa, ob, oc, od, buf, sems):
+    pairs = ((a, oa), (b, ob), (c, oc), (d, od))
+    loads = [pltpu.make_async_copy(src, buf.at[i], sems.at[0, i]) for i, (src, _) in enumerate(pairs)]
+    for cp in loads:
+        cp.start()
+    stores = []
+    for i, (_, dst) in enumerate(pairs):
+        loads[i].wait()
+        cp = pltpu.make_async_copy(buf.at[i], dst, sems.at[1, i])
+        cp.start()
+        stores.append(cp)
+    for cp in stores:
+        cp.wait()
 
 
 def shards(query_tok, key_tok, value_tok, grad_out, decay_rate):
@@ -283,8 +293,9 @@
     return pl.pallas_call(
         settle_kernel,
         out_shape=(out, out, out, out),
-        in_specs=[vspec] * 4,
-        out_specs=(vspec, vspec, vspec, vspec),
+        in_specs=[anyspec] * 4,
+        out_specs=(anyspec, anyspec, anyspec, anyspec),
+        scratch_shapes=[pltpu.VMEM((4,) + out.shape, out.dtype), pltpu.SemaphoreType.DMA((2, 4))],
     )(*moved)
 
 

time: 97.2 us -> 96.9 us (level)
  no operation moved by 1% of the time
where the time goes in v13:
time: 96.9 us; the launch traced here: 96.7 us
  Pallas kernels  95.9 us (99%)
    pallas_call x1, Pallas kernels, shards(): pl.pallas_call(functools.partial(whole_kernel, n, near, far, d, total_len...  93.5 us
    pallas_call x1, Pallas kernels, shards(): pl.pallas_call(settle_kernel, out_shape=(out, out, out, out), in_specs=[a...  2.42 us

profile of v13, /device:TPU:1, one launch (start us, length us, event | category | flops | bytes accessed | tf_op | source)
XLA Modules:
  0.0 96.7 jit_solution(18020341837806807585)
XLA Ops:
  0.6 93.5 %shard_map.84 = (bf16[64,4096]{1,0:T(8,128)(2,1)}, bf16[64,4096]{1,0:T(8,128)(2,1)}, bf16[64,4096]{1,0:T(8,128)(2,1)}, bf16[64,4096]{1,0:T(8,128)(2,1)}) custom-call(f32[2]{0:T(128)} %dec_ref.1, bf16[1024,256]{1,0:T(8,128)(2,1)} %q_ref.1, bf16[1024,256]{1,0:T(8,128)(2,1)} %k_ref.1, bf16[1024,256]{1,0:T(8,128)(2,1)} %v_ref.1, bf16[1024,256]{1,0:T(8,128)(2,1)} %do_ref.1), custom_call_target="tpu_custom_call" | custom-call | tf_op jit(solution)/shard_map/pallas_call | solution.py:266
  94.2 2.4 %shard_map.85 = (bf16[64,4096]{1,0:T(8,128)(2,1)}, bf16[64,4096]{1,0:T(8,128)(2,1)}, bf16[64,4096]{1,0:T(8,128)(2,1)}, bf16[64,4096]{1,0:T(8,128)(2,1)}) custom-call(bf16[64,4096]{1,0:T(8,128)(2,1)} %get-tuple-element.8.a, bf16[64,4096]{1,0:T(8,128)(2,1)} %get-tuple-element.9.b, bf16[64,4096]{1,0:T(8,128)(2,1)} %get-tuple-element.10.c, ...), custom_call_target="tpu_custom_call" | custom-call | tf_op jit(solution)/shard_map/pallas_call | solution.py:293

commit v14 on v12

--- a/solution.py
+++ b/solution.py
@@ -36,12 +36,16 @@
     scales = [jnp.sqrt((2.0 * rates[h] + 2.0 / total) / hd) for h in range(heads)]
     wv = [[jnp.exp(-float(d) * (rates[h] * float(length))) for h in range(heads)] for d in near + [top]]
     place = lax.broadcasted_iota(jnp.int32, (length, 1), 0).astype(f32)
-    for h in range(heads):
-        rate = rates[h]
-        keyed = (k_ref[:, cols(h)].astype(f32) * jnp.exp(-rate * (length - place))).astype(jnp.bfloat16)
-        dk_ref[h] = lax.dot_general(keyed, v_ref[:, cols(h)], tn, preferred_element_type=f32)
-        queried = (q_ref[:, cols(h)].astype(f32) * jnp.exp(-rate * (place + 1.0))).astype(jnp.bfloat16)
-        dq_ref[h] = lax.dot_general(queried, do_ref[:, cols(h)], tn, preferred_element_type=f32)
+    def state_task(h):
+        def run():
+            rate = rates[h]
+            keyed = (k_ref[:, cols(h)].astype(f32) * jnp.exp(-rate * (length - place))).astype(jnp.bfloat16)
+            dk_ref[h] = lax.dot_general(keyed, v_ref[:, cols(h)], tn, preferred_element_type=f32)
+            queried = (q_ref[:, cols(h)].astype(f32) * jnp.exp(-rate * (place + 1.0))).astype(jnp.bfloat16)
+            dq_ref[h] = lax.dot_general(queried, do_ref[:, cols(h)], tn, preferred_element_type=f32)
+        return run
+
+    state_task(0)()
 
     barrier = pltpu.get_barrier_semaphore()
     partners = sorted(set(near + [1, far]))
@@ -132,6 +136,8 @@
 
     for h in range(heads):
         mine = [weights_task(h)] + [intra_task(h, o) for o in range(4)]
+        if h == 0:
+            mine = [state_task(g) for g in range(1, heads)] + mine
         per_round = -(-len(mine) // nround)
         kcur, qcur = dk_ref.at[h], dq_ref.at[h]
         for r, d in enumerate(near):

time: 97.2 us -> 96.4 us (level)
  no operation moved by 1% of the time
where the time goes in v14:
time: 96.4 us; the launch traced here: 96.2 us
  Pallas kernels  95.6 us (99%)
    pallas_call x1, Pallas kernels, shards(): pl.pallas_call(functools.partial(whole_kernel, n, near, far, d, total_len...  92.7 us
    pallas_call x1, Pallas kernels, shards(): pl.pallas_call(settle_kernel, out_shape=(out, out, out, out), in_specs=[v...  2.86 us

profile of v14, /device:TPU:1, one launch (start us, length us, event | category | flops | bytes accessed | tf_op | source)
XLA Modules:
  0.0 96.2 jit_solution(12891225797762299614)
XLA Ops:
  0.6 92.7 %shard_map.84 = (bf16[64,4096]{1,0:T(8,128)(2,1)}, bf16[64,4096]{1,0:T(8,128)(2,1)}, bf16[64,4096]{1,0:T(8,128)(2,1)}, bf16[64,4096]{1,0:T(8,128)(2,1)}) custom-call(f32[2]{0:T(128)} %dec_ref.1, bf16[1024,256]{1,0:T(8,128)(2,1)} %q_ref.1, bf16[1024,256]{1,0:T(8,128)(2,1)} %k_ref.1, bf16[1024,256]{1,0:T(8,128)(2,1)} %v_ref.1, bf16[1024,256]{1,0:T(8,128)(2,1)} %do_ref.1), custom_call_target="tpu_custom_call" | custom-call | tf_op jit(solution)/shard_map/pallas_call | solution.py:262
  93.3 2.9 %shard_map.85 = (bf16[64,4096]{1,0:T(8,128)(2,1)}, bf16[64,4096]{1,0:T(8,128)(2,1)}, bf16[64,4096]{1,0:T(8,128)(2,1)}, bf16[64,4096]{1,0:T(8,128)(2,1)}) custom-call(bf16[64,4096]{1,0:T(8,128)(2,1)} %get-tuple-element.8.a, bf16[64,4096]{1,0:T(8,128)(2,1)} %get-tuple-element.9.b, bf16[64,4096]{1,0:T(8,128)(2,1)} %get-tuple-element.10.c, ...), custom_call_target="tpu_custom_call" | custom-call | tf_op jit(solution)/shard_map/pallas_call | solution.py:289

commit v15 on v14

--- a/solution.py
+++ b/solution.py
@@ -45,7 +45,6 @@
             dq_ref[h] = lax.dot_general(queried, do_ref[:, cols(h)], tn, preferred_element_type=f32)
         return run
 
-    state_task(0)()
 
     barrier = pltpu.get_barrier_semaphore()
     partners = sorted(set(near + [1, far]))
@@ -58,6 +57,7 @@
             peers = peers + jnp.logical_and(other >= 0, other < n).astype(jnp.int32)
     for j in range(1, ne):
         pl.semaphore_signal(barrier, 1, device_id=(me_s, lax.rem(me + j, ne)), device_id_type=MESH)
+    state_task(0)()
     pl.semaphore_wait(barrier, peers)
 
     def weights_task(h):

time: 96.4 us -> 96.4 us (level)
  no operation moved by 1% of the time
where the time goes in v15:
time: 96.4 us; the launch traced here: 96.2 us
  Pallas kernels  95.5 us (99%)
    pallas_call x1, Pallas kernels, shards(): pl.pallas_call(functools.partial(whole_kernel, n, near, far, d, total_len...  92.7 us
    pallas_call x1, Pallas kernels, shards(): pl.pallas_call(settle_kernel, out_shape=(out, out, out, out), in_specs=[v...  2.86 us

profile of v15, /device:TPU:1, one launch (start us, length us, event | category | flops | bytes accessed | tf_op | source)
XLA Modules:
  0.0 96.2 jit_solution(5661887728261063924)
XLA Ops:
  0.6 92.7 %shard_map.84 = (bf16[64,4096]{1,0:T(8,128)(2,1)}, bf16[64,4096]{1,0:T(8,128)(2,1)}, bf16[64,4096]{1,0:T(8,128)(2,1)}, bf16[64,4096]{1,0:T(8,128)(2,1)}) custom-call(f32[2]{0:T(128)} %dec_ref.1, bf16[1024,256]{1,0:T(8,128)(2,1)} %q_ref.1, bf16[1024,256]{1,0:T(8,128)(2,1)} %k_ref.1, bf16[1024,256]{1,0:T(8,128)(2,1)} %v_ref.1, bf16[1024,256]{1,0:T(8,128)(2,1)} %do_ref.1), custom_call_target="tpu_custom_call" | custom-call | tf_op jit(solution)/shard_map/pallas_call | solution.py:262
  93.3 2.9 %shard_map.85 = (bf16[64,4096]{1,0:T(8,128)(2,1)}, bf16[64,4096]{1,0:T(8,128)(2,1)}, bf16[64,4096]{1,0:T(8,128)(2,1)}, bf16[64,4096]{1,0:T(8,128)(2,1)}) custom-call(bf16[64,4096]{1,0:T(8,128)(2,1)} %get-tuple-element.8.a, bf16[64,4096]{1,0:T(8,128)(2,1)} %get-tuple-element.9.b, bf16[64,4096]{1,0:T(8,128)(2,1)} %get-tuple-element.10.c, ...), custom_call_target="tpu_custom_call" | custom-call | tf_op jit(solution)/shard_map/pallas_call | solution.py:289
